TPU v7x, 128 devices: a whole 4x4x4 slice. The times are simulated.
128 devices in a mesh: swath: 4 (over z), col: 32 (over x, y, core).
Axes of the slice: x: 4, y: 4, z: 4, core: 2. Of those that a mesh axis runs over, the one named last changes fastest.
Arguments:
- raw_band: float32 [4096, 32768], P('swath', 'col'), may hold values from -6 to 6
- section_offsets: int32 [32, 2], replicated, may hold values from -16 to 16, as said below
Outputs:
- diffused: float32 [4096, 32768], P('swath', 'col')
- defect: float32 [4096, 32768], P('swath', 'col')
Inputs may be any that keep to these rules, and one draw needn't show every extreme that they name: `section_offsets`: row and column shifts of each die; some die has each extreme in each of the two columns.
All inputs are finite; a program needn't handle non-finite values.
Results may differ from a plain program's by a relative error of at most 0.0003.
Values sent between devices are 32-bit elements; how exact they have to be, the bound alone decides.
A program may use at most 128 MiB of HBM per device.

v0:
```python
import jax
import jax.numpy as jnp
from jax import lax
from jax.sharding import PartitionSpec as P

STEPS = 4
MAXOFF = 16


step_rate = 0.2


def extended(cells, sides, width):
    for axis, dim in sides:
        count = lax.axis_size(axis)
        ends = count - 1
        head = lax.slice_in_dim(cells, 0, width, axis=dim)
        tail = lax.slice_in_dim(cells, cells.shape[dim] - width, cells.shape[dim], axis=dim)
        cells = jnp.concatenate(
            [
                lax.ppermute(tail, axis, [(i, (i + 1) % count) for i in range(ends)]),
                cells,
                lax.ppermute(head, axis, [((i + 1) % count, i) for i in range(ends)]),
            ],
            axis=dim,
        )
    return cells


def from_behind(block, axis, distance):
    devices = range(lax.axis_size(axis))
    route = [((i - distance) % len(devices), i) for i in devices]
    return lax.ppermute(block, axis, route)


def conduct_flux(middle, beside):
    differ = beside - middle
    return differ / (1.0 + differ * differ)


def diffuse_masked(bordered, row_valid, col_valid):
    middle = bordered[1:-1, 1:-1]
    flux_sum = conduct_flux(middle, bordered[:-2, 1:-1]) * row_valid[:-2]
    flux_sum = flux_sum + conduct_flux(middle, bordered[2:, 1:-1]) * row_valid[2:]
    flux_sum = flux_sum + conduct_flux(middle, bordered[1:-1, :-2]) * col_valid[:, :-2]
    flux_sum = flux_sum + conduct_flux(middle, bordered[1:-1, 2:]) * col_valid[:, 2:]
    return middle + step_rate * flux_sum


def three_die(aligned, left_block, right_block):
    first_diff = aligned - left_block
    second_diff = aligned - right_block
    return jnp.maximum(jnp.minimum(first_diff, second_diff), 0.0) + jnp.minimum(
        jnp.maximum(first_diff, second_diff), 0.0
    )


def local(raw_band, section_offsets):
    col_count = lax.axis_size("col")
    swath_count = lax.axis_size("swath")
    row_total, die_width = raw_band.shape
    die_tile = lax.all_to_all(raw_band, "col", split_axis=1, concat_axis=1, tiled=True)
    swath_index = lax.axis_index("swath")
    col_index = lax.axis_index("col")
    band_rows = swath_count * row_total
    band_cols = col_count * die_width
    margin = MAXOFF
    current = die_tile
    rows_here = (
        swath_index * row_total - 1 + lax.broadcasted_iota(jnp.int32, (row_total + 2 * 1, 1), 0)
    )
    row_valid = ((rows_here >= 0) & (rows_here < band_rows)).astype(jnp.float32)
    cols_here = (
        col_index * die_width - 1 + lax.broadcasted_iota(jnp.int32, (1, die_width + 2 * 1), 1)
    )
    col_valid = ((cols_here >= 0) & (cols_here < band_cols)).astype(jnp.float32)
    for step_index in range(STEPS):
        bordered = extended(current, (("swath", 0), ("col", 1)), 1)
        current = diffuse_masked(bordered, row_valid, col_valid)
    padded = extended(current, (("swath", 0), ("col", 1)), margin)
    die_ids = lax.broadcasted_iota(jnp.int32, section_offsets.shape, 0)
    own_shift = jnp.sum(jnp.where(die_ids == col_index, section_offsets, 0), axis=0)
    aligned = lax.dynamic_slice(
        padded, (margin + own_shift[0], margin + own_shift[1]), (row_total, die_width)
    )
    left_block = from_behind(aligned, "col", 1)
    right_block = from_behind(aligned, "col", -1)
    defect = three_die(aligned, left_block, right_block)
    return (current, defect)


def solution(mesh):
    in_specs = (P("swath", "col"), P())
    out_specs = (P("swath", "col"), P("swath", "col"))
    return jax.shard_map(local, mesh=mesh, in_specs=in_specs, out_specs=out_specs, check_vma=False)
```

profile of v0, /device:TPU:0, one launch (start us, length us, event | category | flops | bytes accessed | tf_op | source)
XLA Modules:
  0.0 369.5 jit_solution(8573203426081574793)
XLA Ops:
  0.6 5.3 %copy.9 = f32[1024,1024]{0,1:T(8,128)} copy(f32[1024,1024]{1,0:T(8,128)} %param.2) | data formatting | bytes 8388608 | tf_op args[0]
  6.0 7.5 %all-to-all-start = ((f32[1024,32,32]{0,2,1:T(8,128)}), f32[1024,32,32]{0,2,1:T(8,128)}, u32[]{:S(2)}, u32[]{:S(2)}) async-start(f32[1024,32,32]{0,2,1:T(8,128)} %bitcast.12), calls=%async_computation | async-start | bytes 8388608 | tf_op jit(solution)/shard_map/all_to_all | solution.py:62
  13.6 52.7 %all-to-all-done = f32[1024,32,32]{0,2,1:T(8,128)} async-done(((f32[1024,32,32]{0,2,1:T(8,128)}), f32[1024,32,32]{0,2,1:T(8,128)}, u32[]{:S(2)}, u32[]{:S(2)}) %all-to-all-start) | async-done | bytes 4194336 | tf_op jit(solution)/shard_map/all_to_all | solution.py:62
  67.7 3.9 %collective-permute-start = (f32[1,1024]{0,1:T(8,128)S(1)}, f32[1,1024]{0,1:T(8,128)S(1)}, u32[]{:S(2)}, u32[]{:S(2)}) collective-permute-start(f32[1,1024]{0,1:T(8,128)S(1)} %bitcast.14), channel_id=1, source_target_pairs={{0,32},{32,64},{64,96},{1,33},{33,65},{65,97},{2,34},{34,66},{66,9... | collective-permute-start | bytes 12296 | tf_op jit(solution)/shard_map/ppermute | solution.py:21
  72.9 9.6 %collective-permute-done = f32[1,1024]{0,1:T(8,128)S(1)} collective-permute-done((f32[1,1024]{0,1:T(8,128)S(1)}, f32[1,1024]{0,1:T(8,128)S(1)}, u32[]{:S(2)}, u32[]{:S(2)}) %collective-permute-start) | collective-permute-done | bytes 4128 | tf_op jit(solution)/shard_map/ppermute | solution.py:21
  82.5 4.3 %collective-permute-done.1 = f32[1,1024]{0,1:T(8,128)S(1)} collective-permute-done((f32[1,1024]{0,1:T(8,128)S(1)}, f32[1,1024]{0,1:T(8,128)S(1)}, u32[]{:S(2)}, u32[]{:S(2)}) %collective-permute-start.1) | collective-permute-done | bytes 4128 | tf_op jit(solution)/shard_map/ppermute | solution.py:23
  86.8 6.4 %concatenate.72 = f32[1026,1024]{0,1:T(8,128)} concatenate(f32[1,1024]{0,1:T(8,128)S(1)} %collective-permute-done, f32[1024,1024]{0,1:T(8,128)} %bitcast.1, f32[1,1024]{0,1:T(8,128)S(1)} %collective-permute-done.1), dimensions={0} | concatenate | bytes 8404992 | tf_op jit(solution)/shard_map/concatenate | solution.py:19
  96.6 5.4 %collective-permute-done.3 = f32[1026,1]{0,1:T(1,128)S(1)} collective-permute-done((f32[1026,1]{0,1:T(1,128)S(1)}, f32[1026,1]{0,1:T(1,128)S(1)}, u32[]{:S(2)}, u32[]{:S(2)}) %collective-permute-start.3) | collective-permute-done | bytes 4136 | tf_op jit(solution)/shard_map/ppermute | solution.py:23
  102.0 15.0 %multiply_add_fusion.3 = f32[1024,1024]{0,1:T(8,128)S(1)} fusion(f32[1024,1024]{0,1:T(8,128)} %bitcast.1, f32[1026,1]{0,1:T(1,128)S(1)} %collective-permute-done.3, f32[1026,1024]{0,1:T(8,128)} %concatenate.72, f32[1026,1]{0,1:T(1,128)S(1)} %collective-permute-done.2, f32[1,1024]{0,1:T(8,128)S(1)} %collective-permute-done.1, ...), kind=kLoop, calls=%fused_computation.41 | loop fusion | flops 30408704 | bytes 12623888 | tf_op jit(solution)/shard_map/add | solution.py:47
  120.5 4.6 %collective-permute-start.4 = (f32[1,1024]{0,1:T(8,128)S(1)}, f32[1,1024]{0,1:T(8,128)S(1)}, u32[]{:S(2)}, u32[]{:S(2)}) collective-permute-start(f32[1,1024]{0,1:T(8,128)S(1)} %get-tuple-element.23), channel_id=1, source_target_pairs={{0,32},{32,64},{64,96},{1,33},{33,65},{65,97},{2,34},{34,66},{66,9... | collective-permute-start | bytes 12296 | tf_op jit(solution)/shard_map/ppermute | solution.py:21
  125.1 9.4 %collective-permute-done.5 = f32[1,1024]{0,1:T(8,128)S(1)} collective-permute-done((f32[1,1024]{0,1:T(8,128)S(1)}, f32[1,1024]{0,1:T(8,128)S(1)}, u32[]{:S(2)}, u32[]{:S(2)}) %collective-permute-start.5) | collective-permute-done | bytes 4128 | tf_op jit(solution)/shard_map/ppermute | solution.py:23
  136.3 6.4 %concatenate.77 = f32[1026,1024]{0,1:T(8,128)} concatenate(f32[1,1024]{0,1:T(8,128)S(1)} %collective-permute-done.4, f32[1024,1024]{0,1:T(8,128)} %copy-done.2, f32[1,1024]{0,1:T(8,128)S(1)} %collective-permute-done.5), dimensions={0} | concatenate | bytes 8404992 | tf_op jit(solution)/shard_map/concatenate | solution.py:19
  149.6 14.6 %multiply_add_fusion.2 = f32[1024,1024]{0,1:T(8,128)S(1)} fusion(f32[1024,1024]{0,1:T(8,128)} %copy-done.2, f32[1026,1]{0,1:T(1,128)S(1)} %collective-permute-done.7, f32[1026,1024]{0,1:T(8,128)} %concatenate.77, f32[1026,1]{0,1:T(1,128)S(1)} %collective-permute-done.6, f32[1,1024]{0,1:T(8,128)S(1)} %collective-permute-done.5, ...), kind=kLoop, calls=%fused_computation.40 | loop fusion | flops 30408704 | bytes 12623888 | tf_op jit(solution)/shard_map/add | solution.py:47
  167.8 4.8 %collective-permute-start.8 = (f32[1,1024]{0,1:T(8,128)S(1)}, f32[1,1024]{0,1:T(8,128)S(1)}, u32[]{:S(2)}, u32[]{:S(2)}) collective-permute-start(f32[1,1024]{0,1:T(8,128)S(1)} %get-tuple-element.21), channel_id=1, source_target_pairs={{0,32},{32,64},{64,96},{1,33},{33,65},{65,97},{2,34},{34,66},{66,9... | collective-permute-start | bytes 12296 | tf_op jit(solution)/shard_map/ppermute | solution.py:21
  172.5 9.6 %collective-permute-done.9 = f32[1,1024]{0,1:T(8,128)S(1)} collective-permute-done((f32[1,1024]{0,1:T(8,128)S(1)}, f32[1,1024]{0,1:T(8,128)S(1)}, u32[]{:S(2)}, u32[]{:S(2)}) %collective-permute-start.9) | collective-permute-done | bytes 4128 | tf_op jit(solution)/shard_map/ppermute | solution.py:23
  183.9 6.4 %concatenate.82 = f32[1026,1024]{0,1:T(8,128)} concatenate(f32[1,1024]{0,1:T(8,128)S(1)} %collective-permute-done.8, f32[1024,1024]{0,1:T(8,128)} %copy-done.3, f32[1,1024]{0,1:T(8,128)S(1)} %collective-permute-done.9), dimensions={0} | concatenate | bytes 8404992 | tf_op jit(solution)/shard_map/concatenate | solution.py:19
  198.3 14.6 %multiply_add_fusion.1 = f32[1024,1024]{0,1:T(8,128)S(1)} fusion(f32[1024,1024]{0,1:T(8,128)} %copy-done.3, f32[1026,1]{0,1:T(1,128)S(1)} %collective-permute-done.11, f32[1026,1024]{0,1:T(8,128)} %concatenate.82, f32[1026,1]{0,1:T(1,128)S(1)} %collective-permute-done.10, f32[1,1024]{0,1:T(8,128)S(1)} %collective-permute-done.9, ...), kind=kLoop, calls=%fused_computation.39 | loop fusion | flops 30408704 | bytes 12623888 | tf_op jit(solution)/shard_map/add | solution.py:47
  216.5 5.0 %collective-permute-start.12 = (f32[1,1024]{0,1:T(8,128)S(1)}, f32[1,1024]{0,1:T(8,128)S(1)}, u32[]{:S(2)}, u32[]{:S(2)}) collective-permute-start(f32[1,1024]{0,1:T(8,128)S(1)} %get-tuple-element.19), channel_id=1, source_target_pairs={{0,32},{32,64},{64,96},{1,33},{33,65},{65,97},{2,34},{34,66},{66,9... | collective-permute-start | bytes 12296 | tf_op jit(solution)/shard_map/ppermute | solution.py:21
  221.5 9.1 %collective-permute-done.13 = f32[1,1024]{0,1:T(8,128)S(1)} collective-permute-done((f32[1,1024]{0,1:T(8,128)S(1)}, f32[1,1024]{0,1:T(8,128)S(1)}, u32[]{:S(2)}, u32[]{:S(2)}) %collective-permute-start.13) | collective-permute-done | bytes 4128 | tf_op jit(solution)/shard_map/ppermute | solution.py:23
  232.3 6.4 %concatenate.87 = f32[1026,1024]{0,1:T(8,128)} concatenate(f32[1,1024]{0,1:T(8,128)S(1)} %collective-permute-done.12, f32[1024,1024]{0,1:T(8,128)} %copy-done.1, f32[1,1024]{0,1:T(8,128)S(1)} %collective-permute-done.13), dimensions={0} | concatenate | bytes 8404992 | tf_op jit(solution)/shard_map/concatenate | solution.py:19
  239.5 3.5 collective-permute-start.14
  246.9 14.6 %multiply_add_fusion = f32[1024,1024]{0,1:T(8,128)S(1)} fusion(f32[1024,1024]{0,1:T(8,128)} %copy-done.1, f32[1026,1]{0,1:T(1,128)S(1)} %collective-permute-done.15, f32[1026,1024]{0,1:T(8,128)} %concatenate.87, f32[1026,1]{0,1:T(1,128)S(1)} %collective-permute-done.14, f32[1,1024]{0,1:T(8,128)S(1)} %collective-permute-done.13, ...), kind=kLoop, calls=%fused_computation.38 | loop fusion | flops 30408704 | bytes 12623888 | tf_op jit(solution)/shard_map/add | solution.py:47
  265.1 5.0 %collective-permute-start.16 = (f32[16,1024]{0,1:T(8,128)S(1)}, f32[16,1024]{0,1:T(8,128)S(1)}, u32[]{:S(2)}, u32[]{:S(2)}) collective-permute-start(f32[16,1024]{0,1:T(8,128)S(1)} %get-tuple-element.17), channel_id=1, source_target_pairs={{0,32},{32,64},{64,96},{1,33},{33,65},{65,97},{2,34},{34,66},{66,9... | collective-permute-start | bytes 196616 | tf_op jit(solution)/shard_map/ppermute | solution.py:21
  270.3 8.9 %collective-permute-done.17 = f32[16,1024]{0,1:T(8,128)S(1)} collective-permute-done((f32[16,1024]{0,1:T(8,128)S(1)}, f32[16,1024]{0,1:T(8,128)S(1)}, u32[]{:S(2)}, u32[]{:S(2)}) %collective-permute-start.17) | collective-permute-done | bytes 65568 | tf_op jit(solution)/shard_map/ppermute | solution.py:23
  280.9 6.4 %concatenate.90 = f32[1056,1024]{0,1:T(8,128)} concatenate(f32[16,1024]{0,1:T(8,128)S(1)} %collective-permute-done.16, f32[1024,1024]{0,1:T(8,128)} %copy-done, f32[16,1024]{0,1:T(8,128)S(1)} %collective-permute-done.17), dimensions={0} | concatenate | bytes 8650752 | tf_op jit(solution)/shard_map/concatenate | solution.py:19
  289.5 4.1 %collective-permute-start.18 = (f32[1056,16]{0,1:T(8,128)S(1)}, f32[1056,16]{0,1:T(8,128)S(1)}, u32[]{:S(2)}, u32[]{:S(2)}) collective-permute-start(f32[1056,16]{0,1:T(8,128)S(1)} %get-tuple-element.7), channel_id=1, source_target_pairs={{0,1},{1,2},{2,3},{3,4},{4,5},{5,6},{6,7},{7,8},{8,9},{9,10},{10,1... | collective-permute-start | bytes 202760 | tf_op jit(solution)/shard_map/ppermute | solution.py:21
  296.7 7.2 %fusion.1 = f32[1024,1024]{0,1:T(8,128)} fusion(s32[]{:T(128)S(6)} %select_n.11, s32[]{:T(128)S(6)} %select_n.12, f32[1056,16]{0,1:T(8,128)S(1)} %collective-permute-done.18, f32[1056,1024]{0,1:T(8,128)} %concatenate.90, f32[1056,16]{0,1:T(8,128)S(1)} %collective-permute-done.19), kind=kLoop, calls=%fused_computation.4 | loop fusion | flops 2097152 | bytes 8654856 | tf_op jit(solution)/shard_map/concatenate | solution.py:19
  305.7 5.3 %copy.12 = f32[1024,1024]{1,0:T(8,128)} copy(f32[1024,1024]{0,1:T(8,128)} %copy-done) | data formatting | bytes 8388608
  311.0 39.3 %collective-permute-done.21 = f32[1024,1024]{0,1:T(8,128)} collective-permute-done((f32[1024,1024]{0,1:T(8,128)}, f32[1024,1024]{0,1:T(8,128)}, u32[]{:S(2)}, u32[]{:S(2)}) %collective-permute-start.21) | collective-permute-done | bytes 4194336 | tf_op jit(solution)/shard_map/ppermute | solution.py:33
  350.3 5.2 %collective-permute-done.20 = f32[1024,1024]{0,1:T(8,128)} collective-permute-done((f32[1024,1024]{0,1:T(8,128)}, f32[1024,1024]{0,1:T(8,128)}, u32[]{:S(2)}, u32[]{:S(2)}) %collective-permute-start.20) | collective-permute-done | bytes 4194336 | tf_op jit(solution)/shard_map/ppermute | solution.py:33
  355.5 8.7 %minimum_add_fusion = f32[1024,1024]{0,1:T(8,128)} fusion(f32[1024,1024]{0,1:T(8,128)} %fusion.1, f32[1024,1024]{0,1:T(8,128)} %collective-permute-done.21, f32[1024,1024]{0,1:T(8,128)} %collective-permute-done.20), kind=kLoop, calls=%fused_computation.37 | loop fusion | flops 7340032 | bytes 16777216 | tf_op jit(solution)/shard_map/add | solution.py:53
  364.2 5.3 %copy.13 = f32[1024,1024]{1,0:T(8,128)} copy(f32[1024,1024]{0,1:T(8,128)} %minimum_add_fusion) | data formatting | bytes 8388608
  (55 shorter events, 51.8 us)
Async XLA Ops:
  6.0 60.3 %all-to-all-start = ((f32[1024,32,32]{0,2,1:T(8,128)}), f32[1024,32,32]{0,2,1:T(8,128)}, u32[]{:S(2)}, u32[]{:S(2)}) async-start(f32[1024,32,32]{0,2,1:T(8,128)} %bitcast.12), calls=%async_computation | async-start | bytes 8388608 | tf_op jit(solution)/shard_map/all_to_all | solution.py:62
  67.7 14.8 %collective-permute-start = (f32[1,1024]{0,1:T(8,128)S(1)}, f32[1,1024]{0,1:T(8,128)S(1)}, u32[]{:S(2)}, u32[]{:S(2)}) collective-permute-start(f32[1,1024]{0,1:T(8,128)S(1)} %bitcast.14), channel_id=1, source_target_pairs={{0,32},{32,64},{64,96},{1,33},{33,65},{65,97},{2,34},{34,66},{66,9... | collective-permute-start | bytes 12296 | tf_op jit(solution)/shard_map/ppermute | solution.py:21
  71.6 15.2 %collective-permute-start.1 = (f32[1,1024]{0,1:T(8,128)S(1)}, f32[1,1024]{0,1:T(8,128)S(1)}, u32[]{:S(2)}, u32[]{:S(2)}) collective-permute-start(f32[1,1024]{0,1:T(8,128)S(1)} %bitcast.13), channel_id=1, source_target_pairs={{32,0},{64,32},{96,64},{33,1},{65,33},{97,65},{34,2},{66,34},{98,6... | collective-permute-start | bytes 12296 | tf_op jit(solution)/shard_map/ppermute | solution.py:23
  94.0 2.7 collective-permute-start.2
  95.3 6.8 %collective-permute-start.3 = (f32[1026,1]{0,1:T(1,128)S(1)}, f32[1026,1]{0,1:T(1,128)S(1)}, u32[]{:S(2)}, u32[]{:S(2)}) collective-permute-start(f32[1026,1]{0,1:T(1,128)S(1)} %get-tuple-element.15), channel_id=1, source_target_pairs={{1,0},{2,1},{3,2},{4,3},{5,4},{6,5},{7,6},{8,7},{9,8},{10,9},{11,1... | collective-permute-start | bytes 12320 | tf_op jit(solution)/shard_map/ppermute | solution.py:23
  117.0 2.0 copy-start.2
  119.2 15.2 %collective-permute-start.5 = (f32[1,1024]{0,1:T(8,128)S(1)}, f32[1,1024]{0,1:T(8,128)S(1)}, u32[]{:S(2)}, u32[]{:S(2)}) collective-permute-start(f32[1,1024]{0,1:T(8,128)S(1)} %get-tuple-element.22), channel_id=1, source_target_pairs={{32,0},{64,32},{96,64},{33,1},{65,33},{97,65},{34,2},{66,34},{98,6... | collective-permute-start | bytes 12296 | tf_op jit(solution)/shard_map/ppermute | solution.py:23
  120.5 15.7 %collective-permute-start.4 = (f32[1,1024]{0,1:T(8,128)S(1)}, f32[1,1024]{0,1:T(8,128)S(1)}, u32[]{:S(2)}, u32[]{:S(2)}) collective-permute-start(f32[1,1024]{0,1:T(8,128)S(1)} %get-tuple-element.23), channel_id=1, source_target_pairs={{0,32},{32,64},{64,96},{1,33},{33,65},{65,97},{2,34},{34,66},{66,9... | collective-permute-start | bytes 12296 | tf_op jit(solution)/shard_map/ppermute | solution.py:21
  143.4 4.5 %collective-permute-start.6 = (f32[1026,1]{0,1:T(1,128)S(1)}, f32[1026,1]{0,1:T(1,128)S(1)}, u32[]{:S(2)}, u32[]{:S(2)}) collective-permute-start(f32[1026,1]{0,1:T(1,128)S(1)} %get-tuple-element.12), channel_id=1, source_target_pairs={{0,1},{1,2},{2,3},{3,4},{4,5},{5,6},{6,7},{7,8},{8,9},{9,10},{10,1... | collective-permute-start | bytes 12320 | tf_op jit(solution)/shard_map/ppermute | solution.py:21
  146.6 3.1 collective-permute-start.7
  164.3 2.0 copy-start.3
  166.5 15.6 %collective-permute-start.9 = (f32[1,1024]{0,1:T(8,128)S(1)}, f32[1,1024]{0,1:T(8,128)S(1)}, u32[]{:S(2)}, u32[]{:S(2)}) collective-permute-start(f32[1,1024]{0,1:T(8,128)S(1)} %get-tuple-element.20), channel_id=1, source_target_pairs={{32,0},{64,32},{96,64},{33,1},{65,33},{97,65},{34,2},{66,34},{98,6... | collective-permute-start | bytes 12296 | tf_op jit(solution)/shard_map/ppermute | solution.py:23
  167.8 16.1 %collective-permute-start.8 = (f32[1,1024]{0,1:T(8,128)S(1)}, f32[1,1024]{0,1:T(8,128)S(1)}, u32[]{:S(2)}, u32[]{:S(2)}) collective-permute-start(f32[1,1024]{0,1:T(8,128)S(1)} %get-tuple-element.21), channel_id=1, source_target_pairs={{0,32},{32,64},{64,96},{1,33},{33,65},{65,97},{2,34},{34,66},{66,9... | collective-permute-start | bytes 12296 | tf_op jit(solution)/shard_map/ppermute | solution.py:21
  191.1 4.4 %collective-permute-start.10 = (f32[1026,1]{0,1:T(1,128)S(1)}, f32[1026,1]{0,1:T(1,128)S(1)}, u32[]{:S(2)}, u32[]{:S(2)}) collective-permute-start(f32[1026,1]{0,1:T(1,128)S(1)} %get-tuple-element.10), channel_id=1, source_target_pairs={{0,1},{1,2},{2,3},{3,4},{4,5},{5,6},{6,7},{7,8},{8,9},{9,10},{10,1... | collective-permute-start | bytes 12320 | tf_op jit(solution)/shard_map/ppermute | solution.py:21
  194.0 4.3 %collective-permute-start.11 = (f32[1026,1]{0,1:T(1,128)S(1)}, f32[1026,1]{0,1:T(1,128)S(1)}, u32[]{:S(2)}, u32[]{:S(2)}) collective-permute-start(f32[1026,1]{0,1:T(1,128)S(1)} %get-tuple-element.11), channel_id=1, source_target_pairs={{1,0},{2,1},{3,2},{4,3},{5,4},{6,5},{7,6},{8,7},{9,8},{10,9},{11,1... | collective-permute-start | bytes 12320 | tf_op jit(solution)/shard_map/ppermute | solution.py:23
  212.9 2.0 copy-start.1
  215.2 15.4 %collective-permute-start.13 = (f32[1,1024]{0,1:T(8,128)S(1)}, f32[1,1024]{0,1:T(8,128)S(1)}, u32[]{:S(2)}, u32[]{:S(2)}) collective-permute-start(f32[1,1024]{0,1:T(8,128)S(1)} %get-tuple-element.18), channel_id=1, source_target_pairs={{32,0},{64,32},{96,64},{33,1},{65,33},{97,65},{34,2},{66,34},{98,6... | collective-permute-start | bytes 12296 | tf_op jit(solution)/shard_map/ppermute | solution.py:23
  216.5 15.9 %collective-permute-start.12 = (f32[1,1024]{0,1:T(8,128)S(1)}, f32[1,1024]{0,1:T(8,128)S(1)}, u32[]{:S(2)}, u32[]{:S(2)}) collective-permute-start(f32[1,1024]{0,1:T(8,128)S(1)} %get-tuple-element.19), channel_id=1, source_target_pairs={{0,32},{32,64},{64,96},{1,33},{33,65},{65,97},{2,34},{34,66},{66,9... | collective-permute-start | bytes 12296 | tf_op jit(solution)/shard_map/ppermute | solution.py:21
  239.5 4.8 %collective-permute-start.14 = (f32[1026,1]{0,1:T(1,128)S(1)}, f32[1026,1]{0,1:T(1,128)S(1)}, u32[]{:S(2)}, u32[]{:S(2)}) collective-permute-start(f32[1026,1]{0,1:T(1,128)S(1)} %get-tuple-element.8), channel_id=1, source_target_pairs={{0,1},{1,2},{2,3},{3,4},{4,5},{5,6},{6,7},{7,8},{8,9},{9,10},{10,1... | collective-permute-start | bytes 12320 | tf_op jit(solution)/shard_map/ppermute | solution.py:21
  243.0 4.0 %collective-permute-start.15 = (f32[1026,1]{0,1:T(1,128)S(1)}, f32[1026,1]{0,1:T(1,128)S(1)}, u32[]{:S(2)}, u32[]{:S(2)}) collective-permute-start(f32[1026,1]{0,1:T(1,128)S(1)} %get-tuple-element.9), channel_id=1, source_target_pairs={{1,0},{2,1},{3,2},{4,3},{5,4},{6,5},{7,6},{8,7},{9,8},{10,9},{11,1... | collective-permute-start | bytes 12320 | tf_op jit(solution)/shard_map/ppermute | solution.py:23
  244.3 25.9 %copy-start.4 = (s32[32,2]{0,1:T(2,128)S(1)}, s32[32,2]{0,1:T(2,128)}, u32[]{:S(2)}) copy-start(s32[32,2]{0,1:T(2,128)} %param.3) | copy-start | bytes 772
  261.5 2.0 copy-start
  263.8 15.4 %collective-permute-start.17 = (f32[16,1024]{0,1:T(8,128)S(1)}, f32[16,1024]{0,1:T(8,128)S(1)}, u32[]{:S(2)}, u32[]{:S(2)}) collective-permute-start(f32[16,1024]{0,1:T(8,128)S(1)} %get-tuple-element.16), channel_id=1, source_target_pairs={{32,0},{64,32},{96,64},{33,1},{65,33},{97,65},{34,2},{66,34},{98,6... | collective-permute-start | bytes 196616 | tf_op jit(solution)/shard_map/ppermute | solution.py:23
  265.1 15.9 %collective-permute-start.16 = (f32[16,1024]{0,1:T(8,128)S(1)}, f32[16,1024]{0,1:T(8,128)S(1)}, u32[]{:S(2)}, u32[]{:S(2)}) collective-permute-start(f32[16,1024]{0,1:T(8,128)S(1)} %get-tuple-element.17), channel_id=1, source_target_pairs={{0,32},{32,64},{64,96},{1,33},{33,65},{65,97},{2,34},{34,66},{66,9... | collective-permute-start | bytes 196616 | tf_op jit(solution)/shard_map/ppermute | solution.py:21
  288.2 8.5 %collective-permute-start.19 = (f32[1056,16]{0,1:T(8,128)S(1)}, f32[1056,16]{0,1:T(8,128)S(1)}, u32[]{:S(2)}, u32[]{:S(2)}) collective-permute-start(f32[1056,16]{0,1:T(8,128)S(1)} %get-tuple-element.6), channel_id=1, source_target_pairs={{1,0},{2,1},{3,2},{4,3},{5,4},{6,5},{7,6},{8,7},{9,8},{10,9},{11,1... | collective-permute-start | bytes 202760 | tf_op jit(solution)/shard_map/ppermute | solution.py:23
  289.5 7.2 %collective-permute-start.18 = (f32[1056,16]{0,1:T(8,128)S(1)}, f32[1056,16]{0,1:T(8,128)S(1)}, u32[]{:S(2)}, u32[]{:S(2)}) collective-permute-start(f32[1056,16]{0,1:T(8,128)S(1)} %get-tuple-element.7), channel_id=1, source_target_pairs={{0,1},{1,2},{2,3},{3,4},{4,5},{5,6},{6,7},{7,8},{8,9},{9,10},{10,1... | collective-permute-start | bytes 202760 | tf_op jit(solution)/shard_map/ppermute | solution.py:21
  303.9 46.3 %collective-permute-start.21 = (f32[1024,1024]{0,1:T(8,128)}, f32[1024,1024]{0,1:T(8,128)}, u32[]{:S(2)}, u32[]{:S(2)}) collective-permute-start(f32[1024,1024]{0,1:T(8,128)} %fusion.1), channel_id=1, source_target_pairs={{1,0},{2,1},{3,2},{4,3},{5,4},{6,5},{7,6},{8,7},{9,8},{10,9},{11,1... | collective-permute-start | bytes 12582920 | tf_op jit(solution)/shard_map/ppermute | solution.py:33
  303.9 51.6 %collective-permute-start.20 = (f32[1024,1024]{0,1:T(8,128)}, f32[1024,1024]{0,1:T(8,128)}, u32[]{:S(2)}, u32[]{:S(2)}) collective-permute-start(f32[1024,1024]{0,1:T(8,128)} %fusion.1), channel_id=1, source_target_pairs={{31,0},{0,1},{1,2},{2,3},{3,4},{4,5},{5,6},{6,7},{7,8},{8,9},{9,10... | collective-permute-start | bytes 12582920 | tf_op jit(solution)/shard_map/ppermute | solution.py:33
where the time goes:
time: 376 us; the launch traced here: 370 us
  waiting for transfers between devices  168 us (45%)
  other arithmetic  74.9 us (20%)
  local copies, waits for them, and re-layouts  63 us (17%)
  starting transfers between devices  60.6 us (16%)
    add x4, other arithmetic, diffuse_masked(): return middle + step_rate * flux_sum  58.8 us
    ppermute x10, waiting for transfers between devices, extended(): lax.ppermute(head, axis, [((i + 1) % count, i) for i in range(ends)])  53.9 us
    all_to_all x1, waiting for transfers between devices, local(): lax.all_to_all(raw_band, 'col', split_axis=1, concat_axis=1, tiled=True)  52.7 us
    ppermute x2, waiting for transfers between devices, from_behind(): return lax.ppermute(block, axis, route)  44.5 us
    ppermute x10, starting transfers between devices, extended(): lax.ppermute(tail, axis, [(i, (i + 1) % count) for i in range(ends)])  38.2 us
    concatenate x5, local copies, waits for them, and re-layouts, extended(): jnp.concatenate([lax.ppermute(tail, axis, [(i, (i + 1) % count) for i in...  31.8 us
    unnamed x13, local copies, waits for them, and re-layouts  24.1 us
    ppermute x10, waiting for transfers between devices, extended(): lax.ppermute(tail, axis, [(i, (i + 1) % count) for i in range(ends)])  16.7 us
  transfers between devices with their start and end apart: 23, of which 17 were waited for; matrix products, arithmetic and copies ran while one was open for 2% of the time, Pallas kernels for 0%

commit v1 on v0

v1 whole, which is shorter than its diff:
```python
import functools

import jax
import jax.numpy as jnp
from jax import lax
from jax.experimental import pallas as pl
from jax.experimental.pallas import tpu as pltpu
from jax.sharding import PartitionSpec as P

STEPS = 4
MAXOFF = 16
ROWH = 24
COLH = 64
PAD = 8
BLK = 8
step_rate = 0.2


def conduct_flux(differ):
    return differ / (1.0 + differ * differ)


def smooth_kernel(band_rows, band_cols, prm, tile, top, bot, side, diff_out, align_out, a_buf, b_buf, fv_buf):
    rows, width = tile.shape
    ext_w = a_buf.shape[1]
    ext_r = rows + 2 * ROWH
    row_base = prm[0] - ROWH
    col_base = prm[1]
    shift_r = prm[2]
    shift_c = prm[3]
    zeros_pad = jnp.zeros((PAD, ext_w), jnp.float32)
    for buf in (a_buf, b_buf, fv_buf):
        buf[pl.ds(0, PAD), :] = zeros_pad
        buf[pl.ds(PAD + ext_r, PAD), :] = zeros_pad
    a_buf[pl.ds(PAD, ROWH), pl.ds(0, width)] = top[...]
    a_buf[pl.ds(PAD + ROWH, rows), pl.ds(0, width)] = tile[...]
    a_buf[pl.ds(PAD + ROWH + rows, ROWH), pl.ds(0, width)] = bot[...]
    a_buf[pl.ds(PAD, ext_r), pl.ds(width, 2 * COLH)] = side[...]

    lane = lax.broadcasted_iota(jnp.int32, (BLK, ext_w), 1)
    gcol = col_base + lane - jnp.where(lane >= width + COLH, ext_w, 0)
    col_edge = (gcol >= 0) & (gcol <= band_cols - 2)
    sub = lax.broadcasted_iota(jnp.int32, (BLK, ext_w), 0)

    def step(src, dst):
        def body(i, carry):
            r0 = pl.multiple_of(PAD + i * BLK, BLK)
            pair = src[pl.ds(r0, 2 * BLK), :]
            here = pair[:BLK]
            below = pltpu.roll(pair, 2 * BLK - 1, 0)[:BLK]
            grow = row_base + (r0 - PAD) + sub
            row_edge = (grow >= 0) & (grow <= band_rows - 2)
            down = jnp.where(row_edge, conduct_flux(below - here), 0.0)
            fv_buf[pl.ds(r0, BLK), :] = down
            up = pltpu.roll(fv_buf[pl.ds(r0 - BLK, 2 * BLK), :], 1, 0)[BLK:]
            right = pltpu.roll(here, ext_w - 1, 1)
            across = jnp.where(col_edge, conduct_flux(right - here), 0.0)
            left = pltpu.roll(across, 1, 1)
            dst[pl.ds(r0, BLK), :] = here + step_rate * ((down - up) + (across - left))
            return carry
        lax.fori_loop(0, ext_r // BLK, body, 0)

    for k in range(STEPS):
        if k % 2 == 0:
            step(a_buf, b_buf)
        else:
            step(b_buf, a_buf)
    final = a_buf if STEPS % 2 == 0 else b_buf

    diff_out[...] = final[pl.ds(PAD + ROWH, rows), pl.ds(0, width)]

    roll_by = lax.rem(ext_w - shift_c, ext_w)
    gcol_a = col_base + shift_c + lax.broadcasted_iota(jnp.int32, (BLK, width), 1)
    col_in = (gcol_a >= 0) & (gcol_a < band_cols)
    sub_a = lax.broadcasted_iota(jnp.int32, (BLK, width), 0)

    start = PAD + ROWH + shift_r
    start_low = (start // BLK) * BLK
    row_roll = lax.rem(2 * BLK - (start - start_low), 2 * BLK)

    def emit(i, carry):
        r0 = pl.multiple_of(i * BLK, BLK)
        block = final[pl.ds(pl.multiple_of(start_low + r0, BLK), 2 * BLK), :]
        block = pltpu.roll(block, row_roll, 0)[:BLK]
        block = pltpu.roll(block, roll_by, 1)[:, :width]
        grow = prm[0] + shift_r + r0 + sub_a
        keep = col_in & (grow >= 0) & (grow < band_rows)
        align_out[pl.ds(r0, BLK), :] = jnp.where(keep, block, 0.0)
        return carry
    lax.fori_loop(0, rows // BLK, emit, 0)


def smooth(prm, tile, top, bot, side, band_rows, band_cols):
    rows, width = tile.shape
    ext_w = width + 2 * COLH
    buf = pltpu.VMEM((rows + 2 * ROWH + 2 * PAD, ext_w), jnp.float32)
    vspec = pl.BlockSpec(memory_space=pltpu.VMEM)
    return pl.pallas_call(
        functools.partial(smooth_kernel, band_rows, band_cols),
        out_shape=(jax.ShapeDtypeStruct((rows, width), jnp.float32),) * 2,
        in_specs=[pl.BlockSpec(memory_space=pltpu.SMEM)] + [vspec] * 4,
        out_specs=(vspec, vspec),
        scratch_shapes=[buf, buf, buf],
        compiler_params=pltpu.CompilerParams(vmem_limit_bytes=60 * 1024 * 1024),
        cost_estimate=pl.CostEstimate(flops=STEPS * 40 * (rows + 2 * ROWH) * ext_w, bytes_accessed=4 * 3 * rows * width, transcendentals=0),
    )(prm, tile, top, bot, side)


def from_behind(block, axis, distance):
    devices = range(lax.axis_size(axis))
    route = [((i - distance) % len(devices), i) for i in devices]
    return lax.ppermute(block, axis, route)


def from_grid(block, d_swath, d_col):
    swaths, cols = lax.axis_size("swath"), lax.axis_size("col")
    route = []
    for s in range(swaths):
        for c in range(cols):
            t, u = s + d_swath, c + d_col
            if 0 <= t < swaths and 0 <= u < cols:
                route.append((s * cols + c, t * cols + u))
    return lax.ppermute(block, ("swath", "col"), route)


def three_die(aligned, left_block, right_block):
    first_diff = aligned - left_block
    second_diff = aligned - right_block
    return jnp.maximum(jnp.minimum(first_diff, second_diff), 0.0) + jnp.minimum(
        jnp.maximum(first_diff, second_diff), 0.0
    )


def local(raw_band, section_offsets):
    col_count = lax.axis_size("col")
    swath_count = lax.axis_size("swath")
    row_total, die_width = raw_band.shape
    die_tile = lax.all_to_all(raw_band, "col", split_axis=1, concat_axis=1, tiled=True)
    swath_index = lax.axis_index("swath")
    col_index = lax.axis_index("col")
    band_rows = swath_count * row_total
    band_cols = col_count * die_width
    first_rows, last_rows = die_tile[:ROWH], die_tile[-ROWH:]
    first_cols, last_cols = die_tile[:, :COLH], die_tile[:, -COLH:]
    top = from_grid(last_rows, 1, 0)
    bot = from_grid(first_rows, -1, 0)
    right = jnp.concatenate(
        [from_grid(last_rows[:, :COLH], 1, -1), from_grid(first_cols, 0, -1), from_grid(first_rows[:, :COLH], -1, -1)], 0
    )
    left = jnp.concatenate(
        [from_grid(last_rows[:, -COLH:], 1, 1), from_grid(last_cols, 0, 1), from_grid(first_rows[:, -COLH:], -1, 1)], 0
    )
    side = jnp.concatenate([right, left], 1)
    die_ids = lax.broadcasted_iota(jnp.int32, section_offsets.shape, 0)
    own_shift = jnp.sum(jnp.where(die_ids == col_index, section_offsets, 0), axis=0)
    prm = jnp.stack(
        [swath_index * row_total, col_index * die_width, own_shift[0], own_shift[1]]
        + [jnp.int32(0)] * 4
    ).astype(jnp.int32)
    diffused, aligned = smooth(prm, die_tile, top, bot, side, band_rows, band_cols)
    left_block = from_behind(aligned, "col", 1)
    right_block = from_behind(aligned, "col", -1)
    defect = three_die(aligned, left_block, right_block)
    return (diffused, defect)


def solution(mesh):
    in_specs = (P("swath", "col"), P())
    out_specs = (P("swath", "col"), P("swath", "col"))
    return jax.shard_map(local, mesh=mesh, in_specs=in_specs, out_specs=out_specs, check_vma=False)
```

time: 376 us -> 272 us (0.72)
  Pallas kernels: 0 us -> 106 us
  other arithmetic: 74.9 us -> 7.52 us
  waiting for transfers between devices: 168 us -> 108 us
  local copies, waits for them, and re-layouts: 63 us -> 15.3 us
  starting transfers between devices: 60.6 us -> 31.5 us
    pallas_call x0 -> x1, Pallas kernels: none -> 106 us  [smooth(): pl.pallas_call(functools.partial(smooth_kernel, band_rows, band_cols), ou...]
    ppermute x20 -> x8, waiting for transfers between devices: 70.5 us -> 4.84 us  [from_grid(): return lax.ppermute(block, ('swath', 'col'), route)]
    add x4 -> x0, other arithmetic: 58.8 us -> none  [diffuse_masked(): return middle + step_rate * flux_sum]
    concatenate x5 -> x0, local copies, waits for them, and re-layouts: 31.8 us -> none  [extended(): jnp.concatenate([lax.ppermute(tail, axis, [(i, (i + 1) % count) for i in...]
    ppermute x20 -> x8, starting transfers between devices: 51.3 us -> 23.3 us  [from_grid(): return lax.ppermute(block, ('swath', 'col'), route)]
    unnamed x13 -> x7, local copies, waits for them, and re-layouts: 24.1 us -> 5.99 us
    ppermute x2, waiting for transfers between devices: 44.5 us -> 51 us  [from_behind(): return lax.ppermute(block, axis, route)]
    concatenate x1, other arithmetic: 7.22 us -> 1.02 us  [local(): side = jnp.concatenate([right, left], 1)]
  transfers between devices with their start and end apart: 23 -> 11, of which waited for: 17 -> 5; matrix products, arithmetic and copies ran while one was open for 2% -> 2% of each run, Pallas kernels for 0% -> 0%
where the time goes in v1:
time: 272 us; the launch traced here: 269 us
  waiting for transfers between devices  108 us (40%)
  Pallas kernels  106 us (39%)
  starting transfers between devices  31.5 us (12%)
  local copies, waits for them, and re-layouts  15.3 us (6%)
  other arithmetic  7.52 us (3%)
    pallas_call x1, Pallas kernels, smooth(): pl.pallas_call(functools.partial(smooth_kernel, band_rows, band_cols), ou...  106 us
    all_to_all x1, waiting for transfers between devices, local(): lax.all_to_all(raw_band, 'col', split_axis=1, concat_axis=1, tiled=True)  52 us
    ppermute x2, waiting for transfers between devices, from_behind(): return lax.ppermute(block, axis, route)  51 us
    ppermute x8, starting transfers between devices, from_grid(): return lax.ppermute(block, ('swath', 'col'), route)  23.3 us
    all_to_all x1, starting transfers between devices, local(): lax.all_to_all(raw_band, 'col', split_axis=1, concat_axis=1, tiled=True)  7.66 us
    unnamed x7, local copies, waits for them, and re-layouts  5.99 us
    add x1, other arithmetic, three_die(): jnp.maximum(jnp.minimum(first_diff, second_diff), 0.0)  5.76 us
  transfers between devices with their start and end apart: 11, of which 5 were waited for; matrix products, arithmetic and copies ran while one was open for 2% of the time, Pallas kernels for 0%

profile of v1, /device:TPU:0, one launch (start us, length us, event | category | flops | bytes accessed | tf_op | source)
XLA Modules:
  0.0 268.6 jit_solution(5179303931836539234)
XLA Ops:
  0.6 5.3 %copy.4 = f32[1024,1024]{0,1:T(8,128)} copy(f32[1024,1024]{1,0:T(8,128)} %param.2) | data formatting | bytes 8388608 | tf_op args[0]
  6.0 7.7 %all-to-all-start = ((f32[1024,32,32]{0,2,1:T(8,128)}), f32[1024,32,32]{0,2,1:T(8,128)}, u32[]{:S(2)}, u32[]{:S(2)}) async-start(f32[1024,32,32]{0,2,1:T(8,128)} %bitcast.6), calls=%async_computation | async-start | bytes 8388608 | tf_op jit(solution)/shard_map/all_to_all | solution.py:138
  13.7 0.1 select_reduce_fusion
  13.8 0.6 pad_add_fusion.prm
  14.4 52.0 %all-to-all-done = f32[1024,32,32]{0,2,1:T(8,128)} async-done(((f32[1024,32,32]{0,2,1:T(8,128)}), f32[1024,32,32]{0,2,1:T(8,128)}, u32[]{:S(2)}, u32[]{:S(2)}) %all-to-all-start) | async-done | bytes 4194336 | tf_op jit(solution)/shard_map/all_to_all | solution.py:138
  66.4 5.3 %copy.13.tile = f32[1024,1024]{1,0:T(8,128)} copy(f32[1024,1024]{0,1:T(8,128)} %bitcast.3) | data formatting | bytes 8388608 | tf_op jit(solution)/shard_map/all_to_all | solution.py:138
  71.8 0.8 fusion
  72.6 0.7 collective-permute-start.2
  73.3 1.4 fusion.1
  74.7 0.7 collective-permute-start.7
  75.3 8.4 %collective-permute-start.5 = (f32[24,64]{1,0:T(8,128)S(1)}, f32[24,64]{1,0:T(8,128)S(1)}, u32[]{:S(2)}, u32[]{:S(2)}) collective-permute-start(f32[24,64]{1,0:T(8,128)S(1)} %get-tuple-element.8), channel_id=1, source_target_pairs={{0,33},{1,34},{2,35},{3,36},{4,37},{5,38},{6,39},{7,40},{8,41},{9,... | collective-permute-start | bytes 18440 | tf_op jit(solution)/shard_map/ppermute | solution.py:123
  83.8 1.3 collective-permute-start.4
  85.1 1.3 collective-permute-start.3
  86.4 0.0 collective-permute-done.2
  86.4 5.2 %collective-permute-start.6 = (f32[1024,64]{1,0:T(8,128)S(1)}, f32[1024,64]{1,0:T(8,128)S(1)}, u32[]{:S(2)}, u32[]{:S(2)}) collective-permute-start(f32[1024,64]{1,0:T(8,128)S(1)} %get-tuple-element.11), channel_id=1, source_target_pairs={{0,1},{1,2},{2,3},{3,4},{4,5},{5,6},{6,7},{7,8},{8,9},{9,10},{10,1... | collective-permute-start | bytes 786440 | tf_op jit(solution)/shard_map/ppermute | solution.py:123
  91.6 1.4 fusion.2
  93.0 0.2 copy.15
  93.2 0.2 copy.14
  93.4 0.0 collective-permute-done.7
  93.4 4.5 %collective-permute-start = (f32[24,1024]{1,0:T(8,128)S(1)}, f32[24,1024]{1,0:T(8,128)S(1)}, u32[]{:S(2)}, u32[]{:S(2)}) collective-permute-start(f32[24,1024]{1,0:T(8,128)S(1)} %copy.14), channel_id=1, source_target_pairs={{0,32},{1,33},{2,34},{3,35},{4,36},{5,37},{6,38},{7,39},{8,40},{9,... | collective-permute-start | bytes 294920 | tf_op jit(solution)/shard_map/ppermute | solution.py:123
  97.9 1.3 collective-permute-start.1
  99.2 0.0 collective-permute-done.3
  99.2 0.0 collective-permute-done.6
  99.2 1.0 maximum_maximum_fusion.side
  100.2 0.1 collective-permute-done.top
  100.3 4.7 %collective-permute-done.1.bot = f32[24,1024]{1,0:T(8,128)S(1)} collective-permute-done((f32[24,1024]{1,0:T(8,128)S(1)}, f32[24,1024]{1,0:T(8,128)S(1)}, u32[]{:S(2)}, u32[]{:S(2)}) %collective-permute-start.1) | collective-permute-done | bytes 98336 | tf_op jit(solution)/shard_map/ppermute | solution.py:123
  105.0 0.6 copy-done.1
  105.7 105.7 %shard_map.41 = (f32[1024,1024]{1,0:T(8,128)}, f32[1024,1024]{1,0:T(8,128)}) custom-call(s32[8]{0:T(128)} %pad_add_fusion.prm, f32[1024,1024]{1,0:T(8,128)} %copy.13.tile, f32[24,1024]{1,0:T(8,128)} %copy-done, f32[24,1024]{1,0:T(8,128)} %copy-done.1, f32[1072,128]{1,0:T(8,128)} %maximum_maximum_fusion.side), custom_call_target="tpu_custom_call" | custom-call | flops 197591040 | bytes 12582912 | tf_op jit(solution)/shard_map/pallas_call | solution.py:98
  211.4 0.5 collective-permute-start.8
  211.9 45.8 %collective-permute-done.9 = f32[1024,1024]{1,0:T(8,128)S(1)} collective-permute-done((f32[1024,1024]{1,0:T(8,128)}, f32[1024,1024]{1,0:T(8,128)S(1)}, u32[]{:S(2)}, u32[]{:S(2)}) %collective-permute-start.9) | collective-permute-done | bytes 4194336 | tf_op jit(solution)/shard_map/ppermute | solution.py:112
  257.8 5.1 %collective-permute-done.8 = f32[1024,1024]{1,0:T(8,128)S(1)} collective-permute-done((f32[1024,1024]{1,0:T(8,128)}, f32[1024,1024]{1,0:T(8,128)S(1)}, u32[]{:S(2)}, u32[]{:S(2)}) %collective-permute-start.8) | collective-permute-done | bytes 4194336 | tf_op jit(solution)/shard_map/ppermute | solution.py:112
  262.9 5.8 %minimum_add_fusion = f32[1024,1024]{1,0:T(8,128)} fusion(f32[1024,1024]{1,0:T(8,128)} %get-tuple-element.5, f32[1024,1024]{1,0:T(8,128)S(1)} %collective-permute-done.9, f32[1024,1024]{1,0:T(8,128)S(1)} %collective-permute-done.8), kind=kLoop, calls=%fused_computation | loop fusion | flops 7340032 | bytes 16777216 | tf_op jit(solution)/shard_map/add | solution.py:129
  (10 shorter events, 0.0 us)
Async XLA Ops:
  6.0 7.7 %copy-start.2 = (s32[32,2]{0,1:T(2,128)S(1)}, s32[32,2]{0,1:T(2,128)}, u32[]{:S(2)}) copy-start(s32[32,2]{0,1:T(2,128)} %param.3) | copy-start | bytes 772
  6.0 60.4 %all-to-all-start = ((f32[1024,32,32]{0,2,1:T(8,128)}), f32[1024,32,32]{0,2,1:T(8,128)}, u32[]{:S(2)}, u32[]{:S(2)}) async-start(f32[1024,32,32]{0,2,1:T(8,128)} %bitcast.6), calls=%async_computation | async-start | bytes 8388608 | tf_op jit(solution)/shard_map/all_to_all | solution.py:138
  72.6 13.8 %collective-permute-start.2 = (f32[24,64]{1,0:T(8,128)S(1)}, f32[24,64]{1,0:T(8,128)S(1)}, u32[]{:S(2)}, u32[]{:S(2)}) collective-permute-start(f32[24,64]{1,0:T(8,128)S(1)} %get-tuple-element.6), channel_id=1, source_target_pairs={{1,32},{2,33},{3,34},{4,35},{5,36},{6,37},{7,38},{8,39},{9,40},{10... | collective-permute-start | bytes 18440 | tf_op jit(solution)/shard_map/ppermute | solution.py:123
  74.7 18.7 %collective-permute-start.7 = (f32[24,64]{1,0:T(8,128)S(1)}, f32[24,64]{1,0:T(8,128)S(1)}, u32[]{:S(2)}, u32[]{:S(2)}) collective-permute-start(f32[24,64]{1,0:T(8,128)S(1)} %get-tuple-element.7), channel_id=1, source_target_pairs={{32,1},{33,2},{34,3},{35,4},{36,5},{37,6},{38,7},{39,8},{40,9},{41... | collective-permute-start | bytes 18440 | tf_op jit(solution)/shard_map/ppermute | solution.py:123
  75.3 22.5 %collective-permute-start.5 = (f32[24,64]{1,0:T(8,128)S(1)}, f32[24,64]{1,0:T(8,128)S(1)}, u32[]{:S(2)}, u32[]{:S(2)}) collective-permute-start(f32[24,64]{1,0:T(8,128)S(1)} %get-tuple-element.8), channel_id=1, source_target_pairs={{0,33},{1,34},{2,35},{3,36},{4,37},{5,38},{6,39},{7,40},{8,41},{9,... | collective-permute-start | bytes 18440 | tf_op jit(solution)/shard_map/ppermute | solution.py:123
  83.8 15.4 %collective-permute-start.4 = (f32[24,64]{1,0:T(8,128)S(1)}, f32[24,64]{1,0:T(8,128)S(1)}, u32[]{:S(2)}, u32[]{:S(2)}) collective-permute-start(f32[24,64]{1,0:T(8,128)S(1)} %get-tuple-element.9), channel_id=1, source_target_pairs={{33,0},{34,1},{35,2},{36,3},{37,4},{38,5},{39,6},{40,7},{41,8},{42... | collective-permute-start | bytes 18440 | tf_op jit(solution)/shard_map/ppermute | solution.py:123
  85.1 14.1 %collective-permute-start.3 = (f32[1024,64]{1,0:T(8,128)S(1)}, f32[1024,64]{1,0:T(8,128)S(1)}, u32[]{:S(2)}, u32[]{:S(2)}) collective-permute-start(f32[1024,64]{1,0:T(8,128)S(1)} %get-tuple-element.10), channel_id=1, source_target_pairs={{1,0},{2,1},{3,2},{4,3},{5,4},{6,5},{7,6},{8,7},{9,8},{10,9},{11,1... | collective-permute-start | bytes 786440 | tf_op jit(solution)/shard_map/ppermute | solution.py:123
  86.4 12.8 %collective-permute-start.6 = (f32[1024,64]{1,0:T(8,128)S(1)}, f32[1024,64]{1,0:T(8,128)S(1)}, u32[]{:S(2)}, u32[]{:S(2)}) collective-permute-start(f32[1024,64]{1,0:T(8,128)S(1)} %get-tuple-element.11), channel_id=1, source_target_pairs={{0,1},{1,2},{2,3},{3,4},{4,5},{5,6},{6,7},{7,8},{8,9},{9,10},{10,1... | collective-permute-start | bytes 786440 | tf_op jit(solution)/shard_map/ppermute | solution.py:123
  93.4 6.9 %collective-permute-start = (f32[24,1024]{1,0:T(8,128)S(1)}, f32[24,1024]{1,0:T(8,128)S(1)}, u32[]{:S(2)}, u32[]{:S(2)}) collective-permute-start(f32[24,1024]{1,0:T(8,128)S(1)} %copy.14), channel_id=1, source_target_pairs={{0,32},{1,33},{2,34},{3,35},{4,36},{5,37},{6,38},{7,39},{8,40},{9,... | collective-permute-start | bytes 294920 | tf_op jit(solution)/shard_map/ppermute | solution.py:123
  97.9 7.2 %collective-permute-start.1 = (f32[24,1024]{1,0:T(8,128)S(1)}, f32[24,1024]{1,0:T(8,128)S(1)}, u32[]{:S(2)}, u32[]{:S(2)}) collective-permute-start(f32[24,1024]{1,0:T(8,128)S(1)} %copy.15), channel_id=1, source_target_pairs={{32,0},{33,1},{34,2},{35,3},{36,4},{37,5},{38,6},{39,7},{40,8},{41... | collective-permute-start | bytes 294920 | tf_op jit(solution)/shard_map/ppermute | solution.py:123
  100.3 4.7 %copy-start = (f32[24,1024]{1,0:T(8,128)}, f32[24,1024]{1,0:T(8,128)S(1)}, u32[]{:S(2)}) copy-start(f32[24,1024]{1,0:T(8,128)S(1)} %collective-permute-done.top) | copy-start | bytes 294916
  105.0 0.6 copy-start.1
  211.4 46.3 %collective-permute-start.9 = (f32[1024,1024]{1,0:T(8,128)}, f32[1024,1024]{1,0:T(8,128)S(1)}, u32[]{:S(2)}, u32[]{:S(2)}) collective-permute-start(f32[1024,1024]{1,0:T(8,128)} %get-tuple-element.5), channel_id=1, source_target_pairs={{1,0},{2,1},{3,2},{4,3},{5,4},{6,5},{7,6},{8,7},{9,8},{10,9},{11,1... | collective-permute-start | bytes 12582920 | tf_op jit(solution)/shard_map/ppermute | solution.py:112
  211.4 51.5 %collective-permute-start.8 = (f32[1024,1024]{1,0:T(8,128)}, f32[1024,1024]{1,0:T(8,128)S(1)}, u32[]{:S(2)}, u32[]{:S(2)}) collective-permute-start(f32[1024,1024]{1,0:T(8,128)} %get-tuple-element.5), channel_id=1, source_target_pairs={{31,0},{0,1},{1,2},{2,3},{3,4},{4,5},{5,6},{6,7},{7,8},{8,9},{9,10... | collective-permute-start | bytes 12582920 | tf_op jit(solution)/shard_map/ppermute | solution.py:112

commit v2 on v1

--- a/solution.py
+++ b/solution.py
@@ -9,10 +9,10 @@
 
 STEPS = 4
 MAXOFF = 16
-ROWH = 24
+ROWH = 32
 COLH = 64
-PAD = 8
-BLK = 8
+PAD = 64
+BLK = 64
 step_rate = 0.2
 
 

time: 272 us -> 194 us (0.71)
  Pallas kernels: 106 us -> 27.3 us
    pallas_call x1, Pallas kernels: 106 us -> 27.3 us  [smooth(): pl.pallas_call(functools.partial(smooth_kernel, band_rows, band_cols), ou...]
  transfers between devices with their start and end apart: 11 -> 11, of which waited for: 5 -> 5; matrix products, arithmetic and copies ran while one was open for 2% -> 3% of each run, Pallas kernels for 0% -> 0%
where the time goes in v2:
time: 194 us; the launch traced here: 191 us
  waiting for transfers between devices  109 us (56%)
  starting transfers between devices  31.5 us (16%)
  Pallas kernels  27.3 us (14%)
  local copies, waits for them, and re-layouts  15.4 us (8%)
  other arithmetic  7.49 us (4%)
    all_to_all x1, waiting for transfers between devices, local(): lax.all_to_all(raw_band, 'col', split_axis=1, concat_axis=1, tiled=True)  52 us
    ppermute x2, waiting for transfers between devices, from_behind(): return lax.ppermute(block, axis, route)  51 us
    pallas_call x1, Pallas kernels, smooth(): pl.pallas_call(functools.partial(smooth_kernel, band_rows, band_cols), ou...  27.3 us
    ppermute x8, starting transfers between devices, from_grid(): return lax.ppermute(block, ('swath', 'col'), route)  23.3 us
    all_to_all x1, starting transfers between devices, local(): lax.all_to_all(raw_band, 'col', split_axis=1, concat_axis=1, tiled=True)  7.66 us
    unnamed x7, local copies, waits for them, and re-layouts  6.01 us
    add x1, other arithmetic, three_die(): jnp.maximum(jnp.minimum(first_diff, second_diff), 0.0)  5.76 us
    ppermute x8, waiting for transfers between devices, from_grid(): return lax.ppermute(block, ('swath', 'col'), route)  5.54 us
  transfers between devices with their start and end apart: 11, of which 5 were waited for; matrix products, arithmetic and copies ran while one was open for 3% of the time, Pallas kernels for 0%

profile of v2, /device:TPU:0, one launch (start us, length us, event | category | flops | bytes accessed | tf_op | source)
XLA Modules:
  0.0 190.9 jit_solution(7324781518934827251)
XLA Ops:
  0.6 5.3 %copy.4 = f32[1024,1024]{0,1:T(8,128)} copy(f32[1024,1024]{1,0:T(8,128)} %param.2) | data formatting | bytes 8388608 | tf_op args[0]
  6.0 7.7 %all-to-all-start = ((f32[1024,32,32]{0,2,1:T(8,128)}), f32[1024,32,32]{0,2,1:T(8,128)}, u32[]{:S(2)}, u32[]{:S(2)}) async-start(f32[1024,32,32]{0,2,1:T(8,128)} %bitcast.6), calls=%async_computation | async-start | bytes 8388608 | tf_op jit(solution)/shard_map/all_to_all | solution.py:138
  13.7 0.1 select_reduce_fusion
  13.8 0.6 pad_add_fusion.prm
  14.4 52.0 %all-to-all-done = f32[1024,32,32]{0,2,1:T(8,128)} async-done(((f32[1024,32,32]{0,2,1:T(8,128)}), f32[1024,32,32]{0,2,1:T(8,128)}, u32[]{:S(2)}, u32[]{:S(2)}) %all-to-all-start) | async-done | bytes 4194336 | tf_op jit(solution)/shard_map/all_to_all | solution.py:138
  66.4 5.3 %copy.13.tile = f32[1024,1024]{1,0:T(8,128)} copy(f32[1024,1024]{0,1:T(8,128)} %bitcast.3) | data formatting | bytes 8388608 | tf_op jit(solution)/shard_map/all_to_all | solution.py:138
  71.8 0.8 fusion
  72.6 0.7 collective-permute-start.2
  73.3 1.4 fusion.1
  74.7 0.7 collective-permute-start.7
  75.3 8.4 %collective-permute-start.5 = (f32[32,64]{1,0:T(8,128)S(1)}, f32[32,64]{1,0:T(8,128)S(1)}, u32[]{:S(2)}, u32[]{:S(2)}) collective-permute-start(f32[32,64]{1,0:T(8,128)S(1)} %get-tuple-element.8), channel_id=1, source_target_pairs={{0,33},{1,34},{2,35},{3,36},{4,37},{5,38},{6,39},{7,40},{8,41},{9,... | collective-permute-start | bytes 24584 | tf_op jit(solution)/shard_map/ppermute | solution.py:123
  83.8 1.3 collective-permute-start.4
  85.1 1.3 collective-permute-start.3
  86.4 0.0 collective-permute-done.2
  86.4 5.2 %collective-permute-start.6 = (f32[1024,64]{1,0:T(8,128)S(1)}, f32[1024,64]{1,0:T(8,128)S(1)}, u32[]{:S(2)}, u32[]{:S(2)}) collective-permute-start(f32[1024,64]{1,0:T(8,128)S(1)} %get-tuple-element.11), channel_id=1, source_target_pairs={{0,1},{1,2},{2,3},{3,4},{4,5},{5,6},{6,7},{7,8},{8,9},{9,10},{10,1... | collective-permute-start | bytes 786440 | tf_op jit(solution)/shard_map/ppermute | solution.py:123
  91.6 1.4 fusion.2
  93.0 0.2 copy.15
  93.2 0.2 copy.14
  93.4 0.0 collective-permute-done.7
  93.4 4.5 %collective-permute-start = (f32[32,1024]{1,0:T(8,128)S(1)}, f32[32,1024]{1,0:T(8,128)S(1)}, u32[]{:S(2)}, u32[]{:S(2)}) collective-permute-start(f32[32,1024]{1,0:T(8,128)S(1)} %copy.14), channel_id=1, source_target_pairs={{0,32},{1,33},{2,34},{3,35},{4,36},{5,37},{6,38},{7,39},{8,40},{9,... | collective-permute-start | bytes 393224 | tf_op jit(solution)/shard_map/ppermute | solution.py:123
  97.9 0.0 collective-permute-done.5
  97.9 1.3 collective-permute-start.1
  99.2 0.0 collective-permute-done.4
  99.2 1.0 maximum_maximum_fusion.side
  100.2 0.8 collective-permute-done.top
  101.0 4.7 %collective-permute-done.1.bot = f32[32,1024]{1,0:T(8,128)S(1)} collective-permute-done((f32[32,1024]{1,0:T(8,128)S(1)}, f32[32,1024]{1,0:T(8,128)S(1)}, u32[]{:S(2)}, u32[]{:S(2)}) %collective-permute-start.1) | collective-permute-done | bytes 131104 | tf_op jit(solution)/shard_map/ppermute | solution.py:123
  105.8 0.7 copy-done.1
  106.4 27.3 %shard_map.41 = (f32[1024,1024]{1,0:T(8,128)}, f32[1024,1024]{1,0:T(8,128)}) custom-call(s32[8]{0:T(128)} %pad_add_fusion.prm, f32[1024,1024]{1,0:T(8,128)} %copy.13.tile, f32[32,1024]{1,0:T(8,128)} %copy-done, f32[32,1024]{1,0:T(8,128)} %copy-done.1, f32[1088,128]{1,0:T(8,128)} %maximum_maximum_fusion.side), custom_call_target="tpu_custom_call" | custom-call | flops 200540160 | bytes 12582912 | tf_op jit(solution)/shard_map/pallas_call | solution.py:98
  133.7 0.5 collective-permute-start.8
  134.2 45.8 %collective-permute-done.9 = f32[1024,1024]{1,0:T(8,128)S(1)} collective-permute-done((f32[1024,1024]{1,0:T(8,128)}, f32[1024,1024]{1,0:T(8,128)S(1)}, u32[]{:S(2)}, u32[]{:S(2)}) %collective-permute-start.9) | collective-permute-done | bytes 4194336 | tf_op jit(solution)/shard_map/ppermute | solution.py:112
  180.1 5.1 %collective-permute-done.8 = f32[1024,1024]{1,0:T(8,128)S(1)} collective-permute-done((f32[1024,1024]{1,0:T(8,128)}, f32[1024,1024]{1,0:T(8,128)S(1)}, u32[]{:S(2)}, u32[]{:S(2)}) %collective-permute-start.8) | collective-permute-done | bytes 4194336 | tf_op jit(solution)/shard_map/ppermute | solution.py:112
  185.2 5.8 %minimum_add_fusion = f32[1024,1024]{1,0:T(8,128)} fusion(f32[1024,1024]{1,0:T(8,128)} %get-tuple-element.5, f32[1024,1024]{1,0:T(8,128)S(1)} %collective-permute-done.9, f32[1024,1024]{1,0:T(8,128)S(1)} %collective-permute-done.8), kind=kLoop, calls=%fused_computation | loop fusion | flops 7340032 | bytes 16777216 | tf_op jit(solution)/shard_map/add | solution.py:129
  (10 shorter events, 0.0 us)
Async XLA Ops:
  6.0 7.7 %copy-start.2 = (s32[32,2]{0,1:T(2,128)S(1)}, s32[32,2]{0,1:T(2,128)}, u32[]{:S(2)}) copy-start(s32[32,2]{0,1:T(2,128)} %param.3) | copy-start | bytes 772
  6.0 60.4 %all-to-all-start = ((f32[1024,32,32]{0,2,1:T(8,128)}), f32[1024,32,32]{0,2,1:T(8,128)}, u32[]{:S(2)}, u32[]{:S(2)}) async-start(f32[1024,32,32]{0,2,1:T(8,128)} %bitcast.6), calls=%async_computation | async-start | bytes 8388608 | tf_op jit(solution)/shard_map/all_to_all | solution.py:138
  72.6 13.8 %collective-permute-start.2 = (f32[32,64]{1,0:T(8,128)S(1)}, f32[32,64]{1,0:T(8,128)S(1)}, u32[]{:S(2)}, u32[]{:S(2)}) collective-permute-start(f32[32,64]{1,0:T(8,128)S(1)} %get-tuple-element.6), channel_id=1, source_target_pairs={{1,32},{2,33},{3,34},{4,35},{5,36},{6,37},{7,38},{8,39},{9,40},{10... | collective-permute-start | bytes 24584 | tf_op jit(solution)/shard_map/ppermute | solution.py:123
  74.7 18.7 %collective-permute-start.7 = (f32[32,64]{1,0:T(8,128)S(1)}, f32[32,64]{1,0:T(8,128)S(1)}, u32[]{:S(2)}, u32[]{:S(2)}) collective-permute-start(f32[32,64]{1,0:T(8,128)S(1)} %get-tuple-element.7), channel_id=1, source_target_pairs={{32,1},{33,2},{34,3},{35,4},{36,5},{37,6},{38,7},{39,8},{40,9},{41... | collective-permute-start | bytes 24584 | tf_op jit(solution)/shard_map/ppermute | solution.py:123
  75.3 22.5 %collective-permute-start.5 = (f32[32,64]{1,0:T(8,128)S(1)}, f32[32,64]{1,0:T(8,128)S(1)}, u32[]{:S(2)}, u32[]{:S(2)}) collective-permute-start(f32[32,64]{1,0:T(8,128)S(1)} %get-tuple-element.8), channel_id=1, source_target_pairs={{0,33},{1,34},{2,35},{3,36},{4,37},{5,38},{6,39},{7,40},{8,41},{9,... | collective-permute-start | bytes 24584 | tf_op jit(solution)/shard_map/ppermute | solution.py:123
  83.8 15.4 %collective-permute-start.4 = (f32[32,64]{1,0:T(8,128)S(1)}, f32[32,64]{1,0:T(8,128)S(1)}, u32[]{:S(2)}, u32[]{:S(2)}) collective-permute-start(f32[32,64]{1,0:T(8,128)S(1)} %get-tuple-element.9), channel_id=1, source_target_pairs={{33,0},{34,1},{35,2},{36,3},{37,4},{38,5},{39,6},{40,7},{41,8},{42... | collective-permute-start | bytes 24584 | tf_op jit(solution)/shard_map/ppermute | solution.py:123
  85.1 14.1 %collective-permute-start.3 = (f32[1024,64]{1,0:T(8,128)S(1)}, f32[1024,64]{1,0:T(8,128)S(1)}, u32[]{:S(2)}, u32[]{:S(2)}) collective-permute-start(f32[1024,64]{1,0:T(8,128)S(1)} %get-tuple-element.10), channel_id=1, source_target_pairs={{1,0},{2,1},{3,2},{4,3},{5,4},{6,5},{7,6},{8,7},{9,8},{10,9},{11,1... | collective-permute-start | bytes 786440 | tf_op jit(solution)/shard_map/ppermute | solution.py:123
  86.4 12.8 %collective-permute-start.6 = (f32[1024,64]{1,0:T(8,128)S(1)}, f32[1024,64]{1,0:T(8,128)S(1)}, u32[]{:S(2)}, u32[]{:S(2)}) collective-permute-start(f32[1024,64]{1,0:T(8,128)S(1)} %get-tuple-element.11), channel_id=1, source_target_pairs={{0,1},{1,2},{2,3},{3,4},{4,5},{5,6},{6,7},{7,8},{8,9},{9,10},{10,1... | collective-permute-start | bytes 786440 | tf_op jit(solution)/shard_map/ppermute | solution.py:123
  93.4 7.6 %collective-permute-start = (f32[32,1024]{1,0:T(8,128)S(1)}, f32[32,1024]{1,0:T(8,128)S(1)}, u32[]{:S(2)}, u32[]{:S(2)}) collective-permute-start(f32[32,1024]{1,0:T(8,128)S(1)} %copy.14), channel_id=1, source_target_pairs={{0,32},{1,33},{2,34},{3,35},{4,36},{5,37},{6,38},{7,39},{8,40},{9,... | collective-permute-start | bytes 393224 | tf_op jit(solution)/shard_map/ppermute | solution.py:123
  97.9 7.9 %collective-permute-start.1 = (f32[32,1024]{1,0:T(8,128)S(1)}, f32[32,1024]{1,0:T(8,128)S(1)}, u32[]{:S(2)}, u32[]{:S(2)}) collective-permute-start(f32[32,1024]{1,0:T(8,128)S(1)} %copy.15), channel_id=1, source_target_pairs={{32,0},{33,1},{34,2},{35,3},{36,4},{37,5},{38,6},{39,7},{40,8},{41... | collective-permute-start | bytes 393224 | tf_op jit(solution)/shard_map/ppermute | solution.py:123
  101.0 4.7 %copy-start = (f32[32,1024]{1,0:T(8,128)}, f32[32,1024]{1,0:T(8,128)S(1)}, u32[]{:S(2)}) copy-start(f32[32,1024]{1,0:T(8,128)S(1)} %collective-permute-done.top) | copy-start | bytes 393220
  105.8 0.7 copy-start.1
  133.7 46.3 %collective-permute-start.9 = (f32[1024,1024]{1,0:T(8,128)}, f32[1024,1024]{1,0:T(8,128)S(1)}, u32[]{:S(2)}, u32[]{:S(2)}) collective-permute-start(f32[1024,1024]{1,0:T(8,128)} %get-tuple-element.5), channel_id=1, source_target_pairs={{1,0},{2,1},{3,2},{4,3},{5,4},{6,5},{7,6},{8,7},{9,8},{10,9},{11,1... | collective-permute-start | bytes 12582920 | tf_op jit(solution)/shard_map/ppermute | solution.py:112
  133.7 51.5 %collective-permute-start.8 = (f32[1024,1024]{1,0:T(8,128)}, f32[1024,1024]{1,0:T(8,128)S(1)}, u32[]{:S(2)}, u32[]{:S(2)}) collective-permute-start(f32[1024,1024]{1,0:T(8,128)} %get-tuple-element.5), channel_id=1, source_target_pairs={{31,0},{0,1},{1,2},{2,3},{3,4},{4,5},{5,6},{6,7},{7,8},{8,9},{9,10... | collective-permute-start | bytes 12582920 | tf_op jit(solution)/shard_map/ppermute | solution.py:112

commit v3 on v2

v3 whole, which is shorter than its diff:
```python
import functools

import jax
import jax.numpy as jnp
from jax import lax
from jax.experimental import pallas as pl
from jax.experimental.pallas import tpu as pltpu
from jax.sharding import PartitionSpec as P

STEPS = 4
MAXOFF = 16
ROWH = 32
COLH = 64
PAD = 64
BLK = 64
step_rate = 0.2


def conduct_flux(differ):
    return differ / (1.0 + differ * differ)


def three_die(aligned, left_block, right_block):
    first_diff = aligned - left_block
    second_diff = aligned - right_block
    return jnp.maximum(jnp.minimum(first_diff, second_diff), 0.0) + jnp.minimum(
        jnp.maximum(first_diff, second_diff), 0.0
    )


def inspect_kernel(
    band_rows, band_cols, prm, tile, top, bot, side, diff_out, defect_out,
    s0, s1, s2, s3, fv_last, held, from_left, from_right, send_sem, recv_sem,
):
    rows, width = tile.shape
    ext_w = s0.shape[1]
    ext_r = rows + 2 * ROWH
    blocks = ext_r // BLK
    out_blocks = rows // BLK
    row_base = prm[0] - ROWH
    col_base = prm[1]
    shift_r = prm[2]
    shift_c = prm[3]
    mesh_ids = pl.DeviceIdType.MESH
    swath = lax.axis_index("swath")
    me = lax.axis_index("col")
    cols = lax.axis_size("col")
    right_dev = lax.rem(me + 1, cols)
    left_dev = lax.rem(me + cols - 1, cols)

    barrier = pltpu.get_barrier_semaphore()
    for partner in (left_dev, right_dev):
        pl.semaphore_signal(barrier, inc=1, device_id=(swath, partner), device_id_type=mesh_ids)
    pl.semaphore_wait(barrier, 2)

    zeros_pad = jnp.zeros((PAD, ext_w), jnp.float32)
    for buf in (s0, s1, s2, s3):
        buf[pl.ds(0, PAD), :] = zeros_pad
        buf[pl.ds(PAD + ext_r, PAD), :] = zeros_pad
    fv_last[...] = jnp.zeros(fv_last.shape, jnp.float32)
    s0[pl.ds(PAD, ROWH), pl.ds(0, width)] = top[...]
    s0[pl.ds(PAD + ROWH, rows), pl.ds(0, width)] = tile[...]
    s0[pl.ds(PAD + ROWH + rows, ROWH), pl.ds(0, width)] = bot[...]
    s0[pl.ds(PAD, ext_r), pl.ds(width, 2 * COLH)] = side[...]

    lane = lax.broadcasted_iota(jnp.int32, (BLK, ext_w), 1)
    gcol = col_base + lane - jnp.where(lane >= width + COLH, ext_w, 0)
    col_edge = (gcol >= 0) & (gcol <= band_cols - 2)
    sub = lax.broadcasted_iota(jnp.int32, (BLK, ext_w), 0)
    stages = (s0, s1, s2, s3, s0)

    def step_block(k, b):
        src, dst = stages[k], stages[k + 1]
        r0 = pl.multiple_of(PAD + b * BLK, BLK)
        pair = src[pl.ds(r0, 2 * BLK), :]
        here = pair[:BLK]
        below = pltpu.roll(pair, 2 * BLK - 1, 0)[:BLK]
        grow = row_base + b * BLK + sub
        row_edge = (grow >= 0) & (grow <= band_rows - 2)
        down = jnp.where(row_edge, conduct_flux(below - here), 0.0)
        above = pltpu.roll(fv_last[k], 1, 0)[0:1]
        up = jnp.where(sub == 0, above, pltpu.roll(down, 1, 0))
        fv_last[k] = down[BLK - 8:]
        right = pltpu.roll(here, ext_w - 1, 1)
        across = jnp.where(col_edge, conduct_flux(right - here), 0.0)
        left = pltpu.roll(across, 1, 1)
        dst[pl.ds(r0, BLK), :] = here + step_rate * ((down - up) + (across - left))

    roll_by = lax.rem(ext_w - shift_c, ext_w)
    gcol_a = col_base + shift_c + lax.broadcasted_iota(jnp.int32, (BLK, width), 1)
    col_in = (gcol_a >= 0) & (gcol_a < band_cols)
    sub_a = lax.broadcasted_iota(jnp.int32, (BLK, width), 0)
    row_roll = 2 * BLK - (ROWH + shift_r)

    def send(a, side_index):
        rows_a = pl.ds(pl.multiple_of(a * BLK, BLK), BLK)
        target = from_left if side_index == 0 else from_right
        return pltpu.make_async_remote_copy(
            src_ref=held.at[rows_a],
            dst_ref=target.at[rows_a],
            send_sem=send_sem.at[side_index, a],
            recv_sem=recv_sem.at[side_index, a],
            device_id=(swath, right_dev if side_index == 0 else left_dev),
            device_id_type=mesh_ids,
        )

    def emit(a):
        r0 = pl.multiple_of(PAD + a * BLK, BLK)
        block = s0[pl.ds(r0, 2 * BLK), :]
        block = pltpu.roll(block, row_roll, 0)[:BLK]
        block = pltpu.roll(block, roll_by, 1)[:, :width]
        grow = prm[0] + shift_r + a * BLK + sub_a
        keep = col_in & (grow >= 0) & (grow < band_rows)
        held[pl.ds(pl.multiple_of(a * BLK, BLK), BLK), :] = jnp.where(keep, block, 0.0)
        send(a, 0).start()
        send(a, 1).start()

    def wave(i, carry):
        for k in range(STEPS):
            b = i - k

            @pl.when((b >= 0) & (b < blocks))
            def _():
                step_block(k, b)

        a = i - STEPS

        @pl.when((a >= 0) & (a < out_blocks))
        def _():
            emit(a)

        return carry

    lax.fori_loop(0, blocks + STEPS, wave, 0)
    diff_out[...] = s0[pl.ds(PAD + ROWH, rows), pl.ds(0, width)]

    def finish(a, carry):
        for side_index in (0, 1):
            send(a, side_index).wait_recv()
        for side_index in (0, 1):
            send(a, side_index).wait_send()
        rows_a = pl.ds(pl.multiple_of(a * BLK, BLK), BLK)
        defect_out[rows_a, :] = three_die(held[rows_a, :], from_left[rows_a, :], from_right[rows_a, :])
        return carry

    lax.fori_loop(0, out_blocks, finish, 0)


def inspect(prm, tile, top, bot, side, band_rows, band_cols):
    rows, width = tile.shape
    ext_w = width + 2 * COLH
    out_blocks = rows // BLK
    buf = pltpu.VMEM((rows + 2 * ROWH + 2 * PAD, ext_w), jnp.float32)
    die = pltpu.VMEM((rows, width), jnp.float32)
    vspec = pl.BlockSpec(memory_space=pltpu.VMEM)
    return pl.pallas_call(
        functools.partial(inspect_kernel, band_rows, band_cols),
        out_shape=(jax.ShapeDtypeStruct((rows, width), jnp.float32),) * 2,
        in_specs=[pl.BlockSpec(memory_space=pltpu.SMEM)] + [vspec] * 4,
        out_specs=(vspec, vspec),
        scratch_shapes=[
            buf, buf, buf, buf,
            pltpu.VMEM((STEPS, 8, ext_w), jnp.float32),
            die, die, die,
            pltpu.SemaphoreType.DMA((2, out_blocks)),
            pltpu.SemaphoreType.DMA((2, out_blocks)),
        ],
        compiler_params=pltpu.CompilerParams(
            vmem_limit_bytes=64000 * 1024, collective_id=0, has_side_effects=True
        ),
        cost_estimate=pl.CostEstimate(
            flops=STEPS * 40 * (rows + 2 * ROWH) * ext_w, bytes_accessed=4 * 3 * rows * width, transcendentals=0
        ),
    )(prm, tile, top, bot, side)


def from_behind(block, axis, distance):
    devices = range(lax.axis_size(axis))
    route = [((i - distance) % len(devices), i) for i in devices]
    return lax.ppermute(block, axis, route)


def from_grid(block, d_swath, d_col):
    swaths, cols = lax.axis_size("swath"), lax.axis_size("col")
    route = []
    for s in range(swaths):
        for c in range(cols):
            t, u = s + d_swath, c + d_col
            if 0 <= t < swaths and 0 <= u < cols:
                route.append((s * cols + c, t * cols + u))
    return lax.ppermute(block, ("swath", "col"), route)


def local(raw_band, section_offsets):
    col_count = lax.axis_size("col")
    swath_count = lax.axis_size("swath")
    row_total, die_width = raw_band.shape
    die_tile = lax.all_to_all(raw_band, "col", split_axis=1, concat_axis=1, tiled=True)
    swath_index = lax.axis_index("swath")
    col_index = lax.axis_index("col")
    band_rows = swath_count * row_total
    band_cols = col_count * die_width
    first_rows, last_rows = die_tile[:ROWH], die_tile[-ROWH:]
    first_cols, last_cols = die_tile[:, :COLH], die_tile[:, -COLH:]
    top = from_grid(last_rows, 1, 0)
    bot = from_grid(first_rows, -1, 0)
    right = jnp.concatenate(
        [from_grid(last_rows[:, :COLH], 1, -1), from_grid(first_cols, 0, -1), from_grid(first_rows[:, :COLH], -1, -1)], 0
    )
    left = jnp.concatenate(
        [from_grid(last_rows[:, -COLH:], 1, 1), from_grid(last_cols, 0, 1), from_grid(first_rows[:, -COLH:], -1, 1)], 0
    )
    side = jnp.concatenate([right, left], 1)
    die_ids = lax.broadcasted_iota(jnp.int32, section_offsets.shape, 0)
    own_shift = jnp.sum(jnp.where(die_ids == col_index, section_offsets, 0), axis=0)
    prm = jnp.stack(
        [swath_index * row_total, col_index * die_width, own_shift[0], own_shift[1]]
        + [jnp.int32(0)] * 4
    ).astype(jnp.int32)
    return inspect(prm, die_tile, top, bot, side, band_rows, band_cols)


def solution(mesh):
    in_specs = (P("swath", "col"), P())
    out_specs = (P("swath", "col"), P("swath", "col"))
    return jax.shard_map(local, mesh=mesh, in_specs=in_specs, out_specs=out_specs, check_vma=False)
```

time: 194 us -> 179 us (0.923)
  waiting for transfers between devices: 109 us -> 56.7 us
  Pallas kernels: 27.3 us -> 62.3 us
  local copies, waits for them, and re-layouts: 15.4 us -> 22.9 us
  other arithmetic: 7.49 us -> 2.52 us
    ppermute x2 -> x0, waiting for transfers between devices: 51 us -> none  [from_behind(): return lax.ppermute(block, axis, route)]
    pallas_call x1, Pallas kernels: 27.3 us -> 62.3 us  [inspect(): pl.pallas_call(functools.partial(inspect_kernel, band_rows, band_cols), o...]
    unnamed x7 -> x11, local copies, waits for them, and re-layouts: 6.01 us -> 12.9 us
    add x1 -> x0, other arithmetic: 5.76 us -> none  [three_die(): jnp.maximum(jnp.minimum(first_diff, second_diff), 0.0)]
  transfers between devices with their start and end apart: 11 -> 9, of which waited for: 5 -> 2; matrix products, arithmetic and copies ran while one was open for 3% -> 3% of each run, Pallas kernels for 0% -> 0%
where the time goes in v3:
time: 179 us; the launch traced here: 176 us
  Pallas kernels  62.3 us (35%)
  waiting for transfers between devices  56.7 us (32%)
  starting transfers between devices  31 us (17%)
  local copies, waits for them, and re-layouts  22.9 us (13%)
  other arithmetic  2.52 us (1%)
    pallas_call x1, Pallas kernels, inspect(): pl.pallas_call(functools.partial(inspect_kernel, band_rows, band_cols), o...  62.3 us
    all_to_all x1, waiting for transfers between devices, local(): lax.all_to_all(raw_band, 'col', split_axis=1, concat_axis=1, tiled=True)  52 us
    ppermute x8, starting transfers between devices, from_grid(): return lax.ppermute(block, ('swath', 'col'), route)  23.3 us
    unnamed x11, local copies, waits for them, and re-layouts  12.9 us
    all_to_all x1, starting transfers between devices, local(): lax.all_to_all(raw_band, 'col', split_axis=1, concat_axis=1, tiled=True)  7.66 us
    all_to_all x1, local copies, waits for them, and re-layouts, local(): lax.all_to_all(raw_band, 'col', split_axis=1, concat_axis=1, tiled=True)  5.34 us
    ppermute x8, waiting for transfers between devices, from_grid(): return lax.ppermute(block, ('swath', 'col'), route)  4.65 us
  transfers between devices with their start and end apart: 9, of which 2 were waited for; matrix products, arithmetic and copies ran while one was open for 3% of the time, Pallas kernels for 0%

profile of v3, /device:TPU:0, one launch (start us, length us, event | category | flops | bytes accessed | tf_op | source)
XLA Modules:
  0.0 176.2 jit_solution(5814905457347051560)
XLA Ops:
  0.6 5.3 %copy.4 = f32[1024,1024]{0,1:T(8,128)} copy(f32[1024,1024]{1,0:T(8,128)} %param.2) | data formatting | bytes 8388608 | tf_op args[0]
  6.0 7.7 %all-to-all-start = ((f32[1024,32,32]{0,2,1:T(8,128)}), f32[1024,32,32]{0,2,1:T(8,128)}, u32[]{:S(2)}, u32[]{:S(2)}) async-start(f32[1024,32,32]{0,2,1:T(8,128)} %bitcast.6), calls=%async_computation | async-start | bytes 8388608 | tf_op jit(solution)/shard_map/all_to_all | solution.py:198
  13.7 0.1 select_reduce_fusion
  13.8 0.6 pad_add_fusion.prm
  14.4 52.0 %all-to-all-done = f32[1024,32,32]{0,2,1:T(8,128)} async-done(((f32[1024,32,32]{0,2,1:T(8,128)}), f32[1024,32,32]{0,2,1:T(8,128)}, u32[]{:S(2)}, u32[]{:S(2)}) %all-to-all-start) | async-done | bytes 4194336 | tf_op jit(solution)/shard_map/all_to_all | solution.py:198
  66.4 5.3 %copy.13.tile = f32[1024,1024]{1,0:T(8,128)} copy(f32[1024,1024]{0,1:T(8,128)} %bitcast.3) | data formatting | bytes 8388608 | tf_op jit(solution)/shard_map/all_to_all | solution.py:198
  71.8 1.4 fusion
  73.2 0.7 collective-permute-start.2
  73.9 1.4 fusion.1
  75.3 1.3 collective-permute-start.7
  76.5 8.4 %collective-permute-start.5 = (f32[32,64]{1,0:T(8,128)S(1)}, f32[32,64]{1,0:T(8,128)}, u32[]{:S(2)}, u32[]{:S(2)}) collective-permute-start(f32[32,64]{1,0:T(8,128)S(1)} %get-tuple-element.4), channel_id=1, source_target_pairs={{0,33},{1,34},{2,35},{3,36},{4,37},{5,38},{6,39},{7,40},{8,41},{9,... | collective-permute-start | bytes 24584 | tf_op jit(solution)/shard_map/ppermute | solution.py:191
  85.0 1.3 collective-permute-start.4
  86.3 1.3 collective-permute-start.3
  87.6 0.0 collective-permute-done.2
  87.6 5.2 %collective-permute-start.6 = (f32[1024,64]{1,0:T(8,128)S(1)}, f32[1024,64]{1,0:T(8,128)S(1)}, u32[]{:S(2)}, u32[]{:S(2)}) collective-permute-start(f32[1024,64]{1,0:T(8,128)S(1)} %get-tuple-element.7), channel_id=1, source_target_pairs={{0,1},{1,2},{2,3},{3,4},{4,5},{5,6},{6,7},{7,8},{8,9},{9,10},{10,1... | collective-permute-start | bytes 786440 | tf_op jit(solution)/shard_map/ppermute | solution.py:191
  92.8 1.4 fusion.2
  94.2 0.2 copy.15
  94.4 0.2 copy.14
  94.6 0.0 collective-permute-done.7
  94.6 3.9 %collective-permute-start = (f32[32,1024]{1,0:T(8,128)S(1)}, f32[32,1024]{1,0:T(8,128)S(1)}, u32[]{:S(2)}, u32[]{:S(2)}) collective-permute-start(f32[32,1024]{1,0:T(8,128)S(1)} %copy.14), channel_id=1, source_target_pairs={{0,32},{1,33},{2,34},{3,35},{4,36},{5,37},{6,38},{7,39},{8,40},{9,... | collective-permute-start | bytes 393224 | tf_op jit(solution)/shard_map/ppermute | solution.py:191
  98.5 0.0 collective-permute-done.5
  98.5 1.3 collective-permute-start.1
  99.8 0.0 collective-permute-done.4
  99.8 0.0 collective-permute-done.3
  99.8 0.0 collective-permute-done.6
  99.8 1.8 %maximum_maximum_fusion.side = f32[1088,128]{1,0:T(8,128)} fusion(f32[32,64]{1,0:T(8,128)} %collective-permute-done.7, f32[1024,64]{1,0:T(8,128)S(1)} %collective-permute-done.6, f32[32,64]{1,0:T(8,128)} %collective-permute-done.5, f32[32,64]{1,0:T(8,128)} %collective-permute-done.4, f32[1024,64]{1,0:T(8,128)S(1)} %collective-permute-done.3, ...), kind=kLoop, calls=%fused_computation | loop fusion | flops 696320 | bytes 1114112 | tf_op jit(solution)/shard_map/concatenate | solution.py:213
  101.6 0.0 collective-permute-done.top
  101.6 4.6 %collective-permute-done.1.bot = f32[32,1024]{1,0:T(8,128)S(1)} collective-permute-done((f32[32,1024]{1,0:T(8,128)S(1)}, f32[32,1024]{1,0:T(8,128)S(1)}, u32[]{:S(2)}, u32[]{:S(2)}) %collective-permute-start.1) | collective-permute-done | bytes 131104 | tf_op jit(solution)/shard_map/ppermute | solution.py:191
  106.2 0.6 copy-done.2
  106.9 62.3 %shard_map.41 = (f32[1024,1024]{1,0:T(8,128)}, f32[1024,1024]{1,0:T(8,128)}) custom-call(s32[8]{0:T(128)} %pad_add_fusion.prm, f32[1024,1024]{1,0:T(8,128)} %copy.13.tile, f32[32,1024]{1,0:T(8,128)} %copy-done.1, f32[32,1024]{1,0:T(8,128)} %copy-done.2, f32[1088,128]{1,0:T(8,128)} %maximum_maximum_fusion.side), custom_call_target="tpu_custom_call" | custom-call | flops 200540160 | bytes 12582912 | tf_op jit(solution)/shard_map/pallas_call | solution.py:156
  169.2 4.9 %copy.18 = f32[1024,1024]{1,0:T(8,128)} copy(f32[1024,1024]{1,0:T(8,128)} %get-tuple-element.12) | data formatting | bytes 8388608
  174.2 2.0 %copy.19 = f32[1024,1024]{1,0:T(8,128)} copy(f32[1024,1024]{1,0:T(8,128)S(1)} %copy-done) | data formatting | bytes 8388608
  (9 shorter events, 0.0 us)
Async XLA Ops:
  6.0 7.7 %copy-start.3 = (s32[32,2]{0,1:T(2,128)S(1)}, s32[32,2]{0,1:T(2,128)}, u32[]{:S(2)}) copy-start(s32[32,2]{0,1:T(2,128)} %param.3) | copy-start | bytes 772
  6.0 60.4 %all-to-all-start = ((f32[1024,32,32]{0,2,1:T(8,128)}), f32[1024,32,32]{0,2,1:T(8,128)}, u32[]{:S(2)}, u32[]{:S(2)}) async-start(f32[1024,32,32]{0,2,1:T(8,128)} %bitcast.6), calls=%async_computation | async-start | bytes 8388608 | tf_op jit(solution)/shard_map/all_to_all | solution.py:198
  73.2 14.4 %collective-permute-start.2 = (f32[32,64]{1,0:T(8,128)S(1)}, f32[32,64]{1,0:T(8,128)S(1)}, u32[]{:S(2)}, u32[]{:S(2)}) collective-permute-start(f32[32,64]{1,0:T(8,128)S(1)} %get-tuple-element.2), channel_id=1, source_target_pairs={{1,32},{2,33},{3,34},{4,35},{5,36},{6,37},{7,38},{8,39},{9,40},{10... | collective-permute-start | bytes 24584 | tf_op jit(solution)/shard_map/ppermute | solution.py:191
  75.3 19.3 %collective-permute-start.7 = (f32[32,64]{1,0:T(8,128)S(1)}, f32[32,64]{1,0:T(8,128)}, u32[]{:S(2)}, u32[]{:S(2)}) collective-permute-start(f32[32,64]{1,0:T(8,128)S(1)} %get-tuple-element.3), channel_id=1, source_target_pairs={{32,1},{33,2},{34,3},{35,4},{36,5},{37,6},{38,7},{39,8},{40,9},{41... | collective-permute-start | bytes 24584 | tf_op jit(solution)/shard_map/ppermute | solution.py:191
  76.5 21.9 %collective-permute-start.5 = (f32[32,64]{1,0:T(8,128)S(1)}, f32[32,64]{1,0:T(8,128)}, u32[]{:S(2)}, u32[]{:S(2)}) collective-permute-start(f32[32,64]{1,0:T(8,128)S(1)} %get-tuple-element.4), channel_id=1, source_target_pairs={{0,33},{1,34},{2,35},{3,36},{4,37},{5,38},{6,39},{7,40},{8,41},{9,... | collective-permute-start | bytes 24584 | tf_op jit(solution)/shard_map/ppermute | solution.py:191
  85.0 14.8 %collective-permute-start.4 = (f32[32,64]{1,0:T(8,128)}, f32[32,64]{1,0:T(8,128)}, u32[]{:S(2)}, u32[]{:S(2)}) collective-permute-start(f32[32,64]{1,0:T(8,128)} %get-tuple-element.5), channel_id=1, source_target_pairs={{33,0},{34,1},{35,2},{36,3},{37,4},{38,5},{39,6},{40,7},{41,8},{42... | collective-permute-start | bytes 24584 | tf_op jit(solution)/shard_map/ppermute | solution.py:191
  86.3 13.5 %collective-permute-start.3 = (f32[1024,64]{1,0:T(8,128)S(1)}, f32[1024,64]{1,0:T(8,128)S(1)}, u32[]{:S(2)}, u32[]{:S(2)}) collective-permute-start(f32[1024,64]{1,0:T(8,128)S(1)} %get-tuple-element.6), channel_id=1, source_target_pairs={{1,0},{2,1},{3,2},{4,3},{5,4},{6,5},{7,6},{8,7},{9,8},{10,9},{11,1... | collective-permute-start | bytes 786440 | tf_op jit(solution)/shard_map/ppermute | solution.py:191
  87.6 12.2 %collective-permute-start.6 = (f32[1024,64]{1,0:T(8,128)S(1)}, f32[1024,64]{1,0:T(8,128)S(1)}, u32[]{:S(2)}, u32[]{:S(2)}) collective-permute-start(f32[1024,64]{1,0:T(8,128)S(1)} %get-tuple-element.7), channel_id=1, source_target_pairs={{0,1},{1,2},{2,3},{3,4},{4,5},{5,6},{6,7},{7,8},{8,9},{9,10},{10,1... | collective-permute-start | bytes 786440 | tf_op jit(solution)/shard_map/ppermute | solution.py:191
  94.6 7.0 %collective-permute-start = (f32[32,1024]{1,0:T(8,128)S(1)}, f32[32,1024]{1,0:T(8,128)S(1)}, u32[]{:S(2)}, u32[]{:S(2)}) collective-permute-start(f32[32,1024]{1,0:T(8,128)S(1)} %copy.14), channel_id=1, source_target_pairs={{0,32},{1,33},{2,34},{3,35},{4,36},{5,37},{6,38},{7,39},{8,40},{9,... | collective-permute-start | bytes 393224 | tf_op jit(solution)/shard_map/ppermute | solution.py:191
  98.5 7.7 %collective-permute-start.1 = (f32[32,1024]{1,0:T(8,128)S(1)}, f32[32,1024]{1,0:T(8,128)S(1)}, u32[]{:S(2)}, u32[]{:S(2)}) collective-permute-start(f32[32,1024]{1,0:T(8,128)S(1)} %copy.15), channel_id=1, source_target_pairs={{32,0},{33,1},{34,2},{35,3},{36,4},{37,5},{38,6},{39,7},{40,8},{41... | collective-permute-start | bytes 393224 | tf_op jit(solution)/shard_map/ppermute | solution.py:191
  101.6 4.6 %copy-start.1 = (f32[32,1024]{1,0:T(8,128)}, f32[32,1024]{1,0:T(8,128)S(1)}, u32[]{:S(2)}) copy-start(f32[32,1024]{1,0:T(8,128)S(1)} %collective-permute-done.top) | copy-start | bytes 393220
  106.2 0.6 copy-start.2
  169.2 5.0 %copy-start = (f32[1024,1024]{1,0:T(8,128)S(1)}, f32[1024,1024]{1,0:T(8,128)}, u32[]{:S(2)}) copy-start(f32[1024,1024]{1,0:T(8,128)} %get-tuple-element.13) | copy-start | bytes 12582916

commit v4 on v3

--- a/solution.py
+++ b/solution.py
@@ -10,7 +10,7 @@
 STEPS = 4
 MAXOFF = 16
 ROWH = 32
-COLH = 64
+COLH = 128
 PAD = 64
 BLK = 64
 step_rate = 0.2
@@ -29,8 +29,8 @@
 
 
 def inspect_kernel(
-    band_rows, band_cols, prm, tile, top, bot, side, diff_out, defect_out,
-    s0, s1, s2, s3, fv_last, held, from_left, from_right, send_sem, recv_sem,
+    band_rows, band_cols, prm, tile, diff_out, defect_out,
+    s0, s1, s2, s3, fv_last, held, from_left, from_right, send_sem, recv_sem, halo_send, halo_recv,
 ):
     rows, width = tile.shape
     ext_w = s0.shape[1]
@@ -45,23 +45,56 @@
     swath = lax.axis_index("swath")
     me = lax.axis_index("col")
     cols = lax.axis_size("col")
+    swaths = lax.axis_size("swath")
     right_dev = lax.rem(me + 1, cols)
     left_dev = lax.rem(me + cols - 1, cols)
+    below_dev = lax.rem(swath + 1, swaths)
+    above_dev = lax.rem(swath + swaths - 1, swaths)
+
+    top_rows, end_rows = pl.ds(0, ROWH), pl.ds(rows - ROWH, ROWH)
+    first_cols, end_cols = pl.ds(0, COLH), pl.ds(width - COLH, COLH)
+    all_rows, all_cols = pl.ds(0, rows), pl.ds(0, width)
+    top_halo, bot_halo, mid_rows = pl.ds(PAD, ROWH), pl.ds(PAD + ROWH + rows, ROWH), pl.ds(PAD + ROWH, rows)
+    right_halo, left_halo = pl.ds(width, COLH), pl.ds(width + COLH, COLH)
+    halo_plan = (
+        ((below_dev, me), (end_rows, all_cols), (top_halo, all_cols)),
+        ((above_dev, me), (top_rows, all_cols), (bot_halo, all_cols)),
+        ((swath, left_dev), (all_rows, first_cols), (mid_rows, right_halo)),
+        ((swath, right_dev), (all_rows, end_cols), (mid_rows, left_halo)),
+        ((below_dev, left_dev), (end_rows, first_cols), (top_halo, right_halo)),
+        ((below_dev, right_dev), (end_rows, end_cols), (top_halo, left_halo)),
+        ((above_dev, left_dev), (top_rows, first_cols), (bot_halo, right_halo)),
+        ((above_dev, right_dev), (top_rows, end_cols), (bot_halo, left_halo)),
+    )
+
+    def halo_copy(n):
+        target, src, dst = halo_plan[n]
+        return pltpu.make_async_remote_copy(
+            src_ref=tile.at[src],
+            dst_ref=s0.at[dst],
+            send_sem=halo_send.at[n],
+            recv_sem=halo_recv.at[n],
+            device_id=target,
+            device_id_type=mesh_ids,
+        )
 
     barrier = pltpu.get_barrier_semaphore()
-    for partner in (left_dev, right_dev):
-        pl.semaphore_signal(barrier, inc=1, device_id=(swath, partner), device_id_type=mesh_ids)
-    pl.semaphore_wait(barrier, 2)
+    for target, _, _ in halo_plan:
+        pl.semaphore_signal(barrier, inc=1, device_id=target, device_id_type=mesh_ids)
+    pl.semaphore_wait(barrier, len(halo_plan))
+    for n in range(len(halo_plan)):
+        halo_copy(n).start()
 
     zeros_pad = jnp.zeros((PAD, ext_w), jnp.float32)
     for buf in (s0, s1, s2, s3):
         buf[pl.ds(0, PAD), :] = zeros_pad
         buf[pl.ds(PAD + ext_r, PAD), :] = zeros_pad
     fv_last[...] = jnp.zeros(fv_last.shape, jnp.float32)
-    s0[pl.ds(PAD, ROWH), pl.ds(0, width)] = top[...]
-    s0[pl.ds(PAD + ROWH, rows), pl.ds(0, width)] = tile[...]
-    s0[pl.ds(PAD + ROWH + rows, ROWH), pl.ds(0, width)] = bot[...]
-    s0[pl.ds(PAD, ext_r), pl.ds(width, 2 * COLH)] = side[...]
+    s0[mid_rows, all_cols] = tile[...]
+    for n in range(len(halo_plan)):
+        halo_copy(n).wait_recv()
+    for n in range(len(halo_plan)):
+        halo_copy(n).wait_send()
 
     lane = lax.broadcasted_iota(jnp.int32, (BLK, ext_w), 1)
     gcol = col_base + lane - jnp.where(lane >= width + COLH, ext_w, 0)
@@ -146,7 +179,7 @@
     lax.fori_loop(0, out_blocks, finish, 0)
 
 
-def inspect(prm, tile, top, bot, side, band_rows, band_cols):
+def inspect(prm, tile, band_rows, band_cols):
     rows, width = tile.shape
     ext_w = width + 2 * COLH
     out_blocks = rows // BLK
@@ -156,7 +189,7 @@
     return pl.pallas_call(
         functools.partial(inspect_kernel, band_rows, band_cols),
         out_shape=(jax.ShapeDtypeStruct((rows, width), jnp.float32),) * 2,
-        in_specs=[pl.BlockSpec(memory_space=pltpu.SMEM)] + [vspec] * 4,
+        in_specs=[pl.BlockSpec(memory_space=pltpu.SMEM), vspec],
         out_specs=(vspec, vspec),
         scratch_shapes=[
             buf, buf, buf, buf,
@@ -164,6 +197,8 @@
             die, die, die,
             pltpu.SemaphoreType.DMA((2, out_blocks)),
             pltpu.SemaphoreType.DMA((2, out_blocks)),
+            pltpu.SemaphoreType.DMA((8,)),
+            pltpu.SemaphoreType.DMA((8,)),
         ],
         compiler_params=pltpu.CompilerParams(
             vmem_limit_bytes=64000 * 1024, collective_id=0, has_side_effects=True
@@ -171,24 +206,7 @@
         cost_estimate=pl.CostEstimate(
             flops=STEPS * 40 * (rows + 2 * ROWH) * ext_w, bytes_accessed=4 * 3 * rows * width, transcendentals=0
         ),
-    )(prm, tile, top, bot, side)
-
-
-def from_behind(block, axis, distance):
-    devices = range(lax.axis_size(axis))
-    route = [((i - distance) % len(devices), i) for i in devices]
-    return lax.ppermute(block, axis, route)
-
-
-def from_grid(block, d_swath, d_col):
-    swaths, cols = lax.axis_size("swath"), lax.axis_size("col")
-    route = []
-    for s in range(swaths):
-        for c in range(cols):
-            t, u = s + d_swath, c + d_col
-            if 0 <= t < swaths and 0 <= u < cols:
-                route.append((s * cols + c, t * cols + u))
-    return lax.ppermute(block, ("swath", "col"), route)
+    )(prm, tile)
 
 
 def local(raw_band, section_offsets):
@@ -200,24 +218,13 @@
     col_index = lax.axis_index("col")
     band_rows = swath_count * row_total
     band_cols = col_count * die_width
-    first_rows, last_rows = die_tile[:ROWH], die_tile[-ROWH:]
-    first_cols, last_cols = die_tile[:, :COLH], die_tile[:, -COLH:]
-    top = from_grid(last_rows, 1, 0)
-    bot = from_grid(first_rows, -1, 0)
-    right = jnp.concatenate(
-        [from_grid(last_rows[:, :COLH], 1, -1), from_grid(first_cols, 0, -1), from_grid(first_rows[:, :COLH], -1, -1)], 0
-    )
-    left = jnp.concatenate(
-        [from_grid(last_rows[:, -COLH:], 1, 1), from_grid(last_cols, 0, 1), from_grid(first_rows[:, -COLH:], -1, 1)], 0
-    )
-    side = jnp.concatenate([right, left], 1)
     die_ids = lax.broadcasted_iota(jnp.int32, section_offsets.shape, 0)
     own_shift = jnp.sum(jnp.where(die_ids == col_index, section_offsets, 0), axis=0)
     prm = jnp.stack(
         [swath_index * row_total, col_index * die_width, own_shift[0], own_shift[1]]
         + [jnp.int32(0)] * 4
     ).astype(jnp.int32)
-    return inspect(prm, die_tile, top, bot, side, band_rows, band_cols)
+    return inspect(prm, die_tile, band_rows, band_cols)
 
 
 def solution(mesh):

time: 179 us -> 153 us (0.85); the launches traced: 176 us -> 152 us
  starting transfers between devices: 31 us -> 7.67 us
  Pallas kernels: 62.3 us -> 73.7 us
  local copies, waits for them, and re-layouts: 22.9 us -> 17.6 us
  waiting for transfers between devices: 56.7 us -> 52 us
  other arithmetic: 2.52 us -> 0.73 us
    ppermute x8 -> x0, starting transfers between devices: 23.3 us -> none  [from_grid(): return lax.ppermute(block, ('swath', 'col'), route)]
    pallas_call x1, Pallas kernels: 62.3 us -> 73.7 us  [inspect(): pl.pallas_call(functools.partial(inspect_kernel, band_rows, band_cols), o...]
    ppermute x8 -> x0, waiting for transfers between devices: 4.65 us -> none  [from_grid(): return lax.ppermute(block, ('swath', 'col'), route)]
    slice x5 -> x0, local copies, waits for them, and re-layouts: 4.61 us -> none  [the longest x3 1.77 us: local(): first_rows, last_rows = (die_tile[:ROWH], die_tile[-ROWH:])]
    unnamed x11 -> x7, local copies, waits for them, and re-layouts: 12.9 us -> 12.3 us
  transfers between devices with their start and end apart: 9 -> 1, of which waited for: 2 -> 1; matrix products, arithmetic and copies ran while one was open for 3% -> 0% of each run, Pallas kernels for 0% -> 0%
where the time goes in v4:
time: 153 us; the launch traced here: 152 us
  Pallas kernels  73.7 us (48%)
  waiting for transfers between devices  52 us (34%)
  local copies, waits for them, and re-layouts  17.6 us (12%)
  starting transfers between devices  7.67 us (5%)
    pallas_call x1, Pallas kernels, inspect(): pl.pallas_call(functools.partial(inspect_kernel, band_rows, band_cols), o...  73.7 us
    all_to_all x1, waiting for transfers between devices, local(): lax.all_to_all(raw_band, 'col', split_axis=1, concat_axis=1, tiled=True)  52 us
    unnamed x7, local copies, waits for them, and re-layouts  12.3 us
    all_to_all x1, starting transfers between devices, local(): lax.all_to_all(raw_band, 'col', split_axis=1, concat_axis=1, tiled=True)  7.67 us
    all_to_all x1, local copies, waits for them, and re-layouts, local(): lax.all_to_all(raw_band, 'col', split_axis=1, concat_axis=1, tiled=True)  5.34 us
  transfers between devices with their start and end apart: 1, of which 1 were waited for; matrix products, arithmetic and copies ran while one was open for 0% of the time, Pallas kernels for 0%

profile of v4, /device:TPU:0, one launch (start us, length us, event | category | flops | bytes accessed | tf_op | source)
XLA Modules:
  0.0 152.4 jit_solution(15856685609039229665)
XLA Ops:
  0.6 5.3 %copy.4 = f32[1024,1024]{0,1:T(8,128)} copy(f32[1024,1024]{1,0:T(8,128)} %param.2) | data formatting | bytes 8388608 | tf_op args[0]
  6.0 0.0 copy-start.1
  6.0 7.7 %all-to-all-start = ((f32[1024,32,32]{0,2,1:T(8,128)}), f32[1024,32,32]{0,2,1:T(8,128)}, u32[]{:S(2)}, u32[]{:S(2)}) async-start(f32[1024,32,32]{0,2,1:T(8,128)} %bitcast.4), calls=%async_computation | async-start | bytes 8388608 | tf_op jit(solution)/shard_map/all_to_all | solution.py:216
  13.7 0.0 copy-done.1
  13.7 0.1 select_reduce_fusion
  13.8 0.6 pad_add_fusion.prm
  14.4 52.0 %all-to-all-done = f32[1024,32,32]{0,2,1:T(8,128)} async-done(((f32[1024,32,32]{0,2,1:T(8,128)}), f32[1024,32,32]{0,2,1:T(8,128)}, u32[]{:S(2)}, u32[]{:S(2)}) %all-to-all-start) | async-done | bytes 4194336 | tf_op jit(solution)/shard_map/all_to_all | solution.py:216
  66.4 5.3 %copy.5.tile = f32[1024,1024]{1,0:T(8,128)} copy(f32[1024,1024]{0,1:T(8,128)} %bitcast.3) | data formatting | bytes 8388608 | tf_op jit(solution)/shard_map/all_to_all | solution.py:216
  71.8 73.7 %shard_map.41 = (f32[1024,1024]{1,0:T(8,128)}, f32[1024,1024]{1,0:T(8,128)}) custom-call(s32[8]{0:T(128)} %pad_add_fusion.prm, f32[1024,1024]{1,0:T(8,128)} %copy.5.tile), custom_call_target="tpu_custom_call" | custom-call | flops 222822400 | bytes 12582912 | tf_op jit(solution)/shard_map/pallas_call | solution.py:189
  145.5 0.0 copy-start
  145.5 4.9 %copy.8 = f32[1024,1024]{1,0:T(8,128)} copy(f32[1024,1024]{1,0:T(8,128)} %get-tuple-element.4) | data formatting | bytes 8388608
  150.4 0.0 copy-done
  150.4 2.0 %copy.9 = f32[1024,1024]{1,0:T(8,128)} copy(f32[1024,1024]{1,0:T(8,128)S(1)} %copy-done) | data formatting | bytes 8388608
  (2 shorter events, 0.0 us)
Async XLA Ops:
  6.0 7.7 %copy-start.1 = (s32[32,2]{0,1:T(2,128)S(1)}, s32[32,2]{0,1:T(2,128)}, u32[]{:S(2)}) copy-start(s32[32,2]{0,1:T(2,128)} %param.3) | copy-start | bytes 772
  6.0 60.5 %all-to-all-start = ((f32[1024,32,32]{0,2,1:T(8,128)}), f32[1024,32,32]{0,2,1:T(8,128)}, u32[]{:S(2)}, u32[]{:S(2)}) async-start(f32[1024,32,32]{0,2,1:T(8,128)} %bitcast.4), calls=%async_computation | async-start | bytes 8388608 | tf_op jit(solution)/shard_map/all_to_all | solution.py:216
  145.5 5.0 %copy-start = (f32[1024,1024]{1,0:T(8,128)S(1)}, f32[1024,1024]{1,0:T(8,128)}, u32[]{:S(2)}) copy-start(f32[1024,1024]{1,0:T(8,128)} %get-tuple-element.5) | copy-start | bytes 12582916

commit v5 on v4

--- a/solution.py
+++ b/solution.py
@@ -29,10 +29,11 @@
 
 
 def inspect_kernel(
-    band_rows, band_cols, prm, tile, diff_out, defect_out,
+    band_rows, band_cols, prm, tile_top, tile_bot, diff_out, defect_out,
     s0, s1, s2, s3, fv_last, held, from_left, from_right, send_sem, recv_sem, halo_send, halo_recv,
 ):
-    rows, width = tile.shape
+    half, width = tile_top.shape
+    rows = 2 * half
     ext_w = s0.shape[1]
     ext_r = rows + 2 * ROWH
     blocks = ext_r // BLK
@@ -51,16 +52,18 @@
     below_dev = lax.rem(swath + 1, swaths)
     above_dev = lax.rem(swath + swaths - 1, swaths)
 
-    top_rows, end_rows = pl.ds(0, ROWH), pl.ds(rows - ROWH, ROWH)
+    top_rows, end_rows = pl.ds(0, ROWH), pl.ds(half - ROWH, ROWH)
     first_cols, end_cols = pl.ds(0, COLH), pl.ds(width - COLH, COLH)
-    all_rows, all_cols = pl.ds(0, rows), pl.ds(0, width)
+    all_rows, all_cols = pl.ds(0, half), pl.ds(0, width)
     top_halo, bot_halo, mid_rows = pl.ds(PAD, ROWH), pl.ds(PAD + ROWH + rows, ROWH), pl.ds(PAD + ROWH, rows)
     right_halo, left_halo = pl.ds(width, COLH), pl.ds(width + COLH, COLH)
     halo_plan = (
         ((below_dev, me), (end_rows, all_cols), (top_halo, all_cols)),
         ((above_dev, me), (top_rows, all_cols), (bot_halo, all_cols)),
-        ((swath, left_dev), (all_rows, first_cols), (mid_rows, right_halo)),
-        ((swath, right_dev), (all_rows, end_cols), (mid_rows, left_halo)),
+        ((swath, left_dev), (all_rows, first_cols), (pl.ds(PAD + ROWH, half), right_halo)),
+        ((swath, right_dev), (all_rows, end_cols), (pl.ds(PAD + ROWH, half), left_halo)),
+        ((swath, left_dev), (all_rows, first_cols), (pl.ds(PAD + ROWH + half, half), right_halo)),
+        ((swath, right_dev), (all_rows, end_cols), (pl.ds(PAD + ROWH + half, half), left_halo)),
         ((below_dev, left_dev), (end_rows, first_cols), (top_halo, right_halo)),
         ((below_dev, right_dev), (end_rows, end_cols), (top_halo, left_halo)),
         ((above_dev, left_dev), (top_rows, first_cols), (bot_halo, right_halo)),
@@ -69,8 +72,10 @@
 
     def halo_copy(n):
         target, src, dst = halo_plan[n]
+        rows_src, cols_src = src
+        tile = tile_bot if n in (0, 4, 5, 6, 7) else tile_top
         return pltpu.make_async_remote_copy(
-            src_ref=tile.at[src],
+            src_ref=tile.at[rows_src, cols_src],
             dst_ref=s0.at[dst],
             send_sem=halo_send.at[n],
             recv_sem=halo_recv.at[n],
@@ -90,7 +95,8 @@
         buf[pl.ds(0, PAD), :] = zeros_pad
         buf[pl.ds(PAD + ext_r, PAD), :] = zeros_pad
     fv_last[...] = jnp.zeros(fv_last.shape, jnp.float32)
-    s0[mid_rows, all_cols] = tile[...]
+    s0[pl.ds(PAD + ROWH, half), all_cols] = tile_top[...]
+    s0[pl.ds(PAD + ROWH + half, half), all_cols] = tile_bot[...]
     for n in range(len(halo_plan)):
         halo_copy(n).wait_recv()
     for n in range(len(halo_plan)):
@@ -179,8 +185,9 @@
     lax.fori_loop(0, out_blocks, finish, 0)
 
 
-def inspect(prm, tile, band_rows, band_cols):
-    rows, width = tile.shape
+def inspect(prm, tile_top, tile_bot, band_rows, band_cols):
+    half, width = tile_top.shape
+    rows = 2 * half
     ext_w = width + 2 * COLH
     out_blocks = rows // BLK
     buf = pltpu.VMEM((rows + 2 * ROWH + 2 * PAD, ext_w), jnp.float32)
@@ -189,7 +196,7 @@
     return pl.pallas_call(
         functools.partial(inspect_kernel, band_rows, band_cols),
         out_shape=(jax.ShapeDtypeStruct((rows, width), jnp.float32),) * 2,
-        in_specs=[pl.BlockSpec(memory_space=pltpu.SMEM), vspec],
+        in_specs=[pl.BlockSpec(memory_space=pltpu.SMEM), vspec, vspec],
         out_specs=(vspec, vspec),
         scratch_shapes=[
             buf, buf, buf, buf,
@@ -197,8 +204,8 @@
             die, die, die,
             pltpu.SemaphoreType.DMA((2, out_blocks)),
             pltpu.SemaphoreType.DMA((2, out_blocks)),
-            pltpu.SemaphoreType.DMA((8,)),
-            pltpu.SemaphoreType.DMA((8,)),
+            pltpu.SemaphoreType.DMA((10,)),
+            pltpu.SemaphoreType.DMA((10,)),
         ],
         compiler_params=pltpu.CompilerParams(
             vmem_limit_bytes=64000 * 1024, collective_id=0, has_side_effects=True
@@ -206,14 +213,18 @@
         cost_estimate=pl.CostEstimate(
             flops=STEPS * 40 * (rows + 2 * ROWH) * ext_w, bytes_accessed=4 * 3 * rows * width, transcendentals=0
         ),
-    )(prm, tile)
+    )(prm, tile_top, tile_bot)
 
 
 def local(raw_band, section_offsets):
     col_count = lax.axis_size("col")
     swath_count = lax.axis_size("swath")
     row_total, die_width = raw_band.shape
-    die_tile = lax.all_to_all(raw_band, "col", split_axis=1, concat_axis=1, tiled=True)
+    half = row_total // 2
+    tile_top, tile_bot = (
+        lax.all_to_all(part, "col", split_axis=1, concat_axis=1, tiled=True)
+        for part in (raw_band[:half], raw_band[half:])
+    )
     swath_index = lax.axis_index("swath")
     col_index = lax.axis_index("col")
     band_rows = swath_count * row_total
@@ -224,7 +235,7 @@
         [swath_index * row_total, col_index * die_width, own_shift[0], own_shift[1]]
         + [jnp.int32(0)] * 4
     ).astype(jnp.int32)
-    return inspect(prm, die_tile, band_rows, band_cols)
+    return inspect(prm, tile_top, tile_bot, band_rows, band_cols)
 
 
 def solution(mesh):

time: 153 us -> 160 us (1.046)
  starting transfers between devices: 7.67 us -> 12.3 us
  local copies, waits for them, and re-layouts: 17.6 us -> 20.4 us
    all_to_all x1 -> x2, starting transfers between devices: 7.67 us -> 12.3 us  [local(): lax.all_to_all(part, 'col', split_axis=1, concat_axis=1, tiled=True)]
    slice x0 -> x1, local copies, waits for them, and re-layouts: none -> 3.99 us  [local(): raw_band[half:]]
    all_to_all x1 -> x2, local copies, waits for them, and re-layouts: 5.34 us -> 4.73 us  [local(): lax.all_to_all(part, 'col', split_axis=1, concat_axis=1, tiled=True)]
    unnamed x7 -> x8, local copies, waits for them, and re-layouts: 12.3 us -> 11.7 us
    all_to_all x1 -> x2, waiting for transfers between devices: 52 us -> 52.3 us  [local(): lax.all_to_all(part, 'col', split_axis=1, concat_axis=1, tiled=True)]
  transfers between devices with their start and end apart: 1 -> 2, of which waited for: 1 -> 2; matrix products, arithmetic and copies ran while one was open for 0% -> 3% of each run, Pallas kernels for 0% -> 0%
where the time goes in v5:
time: 160 us
  Pallas kernels  73.4 us (46%)
  waiting for transfers between devices  52.3 us (33%)
  local copies, waits for them, and re-layouts  20.4 us (13%)
  starting transfers between devices  12.3 us (8%)
    pallas_call x1, Pallas kernels, inspect(): pl.pallas_call(functools.partial(inspect_kernel, band_rows, band_cols), o...  73.4 us
    all_to_all x2, waiting for transfers between devices, local(): lax.all_to_all(part, 'col', split_axis=1, concat_axis=1, tiled=True)  52.3 us
    all_to_all x2, starting transfers between devices, local(): lax.all_to_all(part, 'col', split_axis=1, concat_axis=1, tiled=True)  12.3 us
    unnamed x8, local copies, waits for them, and re-layouts  11.7 us
    all_to_all x2, local copies, waits for them, and re-layouts, local(): lax.all_to_all(part, 'col', split_axis=1, concat_axis=1, tiled=True)  4.73 us
    slice x1, local copies, waits for them, and re-layouts, local(): raw_band[half:]  3.99 us
  transfers between devices with their start and end apart: 2, of which 2 were waited for; matrix products, arithmetic and copies ran while one was open for 3% of the time, Pallas kernels for 0%

profile of v5, /device:TPU:0, one launch (start us, length us, event | category | flops | bytes accessed | tf_op | source)
XLA Modules:
  0.0 159.9 jit_solution(3732418380412316142)
XLA Ops:
  0.6 4.0 %fusion = (f32[512,1024]{1,0:T(8,128)S(1)}, f32[512,1024]{1,0:T(8,128)}) fusion(f32[1024,1024]{1,0:T(8,128)} %param.2), kind=kLoop, calls=%fused_computation.3 | loop fusion | bytes 8388608 | tf_op jit(solution)/shard_map/slice | solution.py:226
  4.6 1.9 %copy.9 = f32[512,1024]{0,1:T(8,128)} copy(f32[512,1024]{1,0:T(8,128)S(1)} %get-tuple-element.2) | data formatting | bytes 4194304
  6.5 7.4 %all-to-all-start.1 = ((f32[512,32,32]{0,2,1:T(8,128)}), f32[512,32,32]{0,2,1:T(8,128)S(1)}, u32[]{:S(2)}, u32[]{:S(2)}) async-start(f32[512,32,32]{0,2,1:T(8,128)} %bitcast.8), calls=%async_computation.1 | async-start | bytes 4194304 | tf_op jit(solution)/shard_map/all_to_all | solution.py:225
  13.9 2.9 %copy.8 = f32[512,1024]{0,1:T(8,128)} copy(f32[512,1024]{1,0:T(8,128)} %get-tuple-element.3) | data formatting | bytes 4194304
  16.8 26.0 %all-to-all-done.1 = f32[512,32,32]{0,2,1:T(8,128)S(1)} async-done(((f32[512,32,32]{0,2,1:T(8,128)}), f32[512,32,32]{0,2,1:T(8,128)S(1)}, u32[]{:S(2)}, u32[]{:S(2)}) %all-to-all-start.1) | async-done | bytes 2097184 | tf_op jit(solution)/shard_map/all_to_all | solution.py:225
  42.8 0.0 copy-start.1
  42.8 4.9 %all-to-all-start = ((f32[512,32,32]{0,2,1:T(8,128)}), f32[512,32,32]{0,2,1:T(8,128)}, u32[]{:S(2)}, u32[]{:S(2)}) async-start(f32[512,32,32]{0,2,1:T(8,128)} %bitcast.7), calls=%async_computation | async-start | bytes 4194304 | tf_op jit(solution)/shard_map/all_to_all | solution.py:225
  47.7 0.0 copy-done.1
  47.8 0.1 select_reduce_fusion
  47.9 0.6 pad_add_fusion.prm
  48.5 1.9 %copy.7.tile_bot = f32[512,1024]{1,0:T(8,128)} copy(f32[512,1024]{0,1:T(8,128)S(1)} %bitcast.6) | data formatting | bytes 4194304 | tf_op jit(solution)/shard_map/all_to_all | solution.py:225
  50.3 26.3 %all-to-all-done = f32[512,32,32]{0,2,1:T(8,128)} async-done(((f32[512,32,32]{0,2,1:T(8,128)}), f32[512,32,32]{0,2,1:T(8,128)}, u32[]{:S(2)}, u32[]{:S(2)}) %all-to-all-start) | async-done | bytes 2097184 | tf_op jit(solution)/shard_map/all_to_all | solution.py:225
  76.6 2.9 %copy.6.tile_top = f32[512,1024]{1,0:T(8,128)} copy(f32[512,1024]{0,1:T(8,128)} %bitcast.3) | data formatting | bytes 4194304 | tf_op jit(solution)/shard_map/all_to_all | solution.py:225
  79.5 73.4 %shard_map.41 = (f32[1024,1024]{1,0:T(8,128)}, f32[1024,1024]{1,0:T(8,128)}) custom-call(s32[8]{0:T(128)} %pad_add_fusion.prm, f32[512,1024]{1,0:T(8,128)} %copy.6.tile_top, f32[512,1024]{1,0:T(8,128)} %copy.7.tile_bot), custom_call_target="tpu_custom_call" | custom-call | flops 222822400 | bytes 12582912 | tf_op jit(solution)/shard_map/pallas_call | solution.py:196
  152.9 0.0 copy-start
  152.9 4.9 %copy.12 = f32[1024,1024]{1,0:T(8,128)} copy(f32[1024,1024]{1,0:T(8,128)} %get-tuple-element.6) | data formatting | bytes 8388608
  157.9 0.0 copy-done
  157.9 2.0 %copy.13 = f32[1024,1024]{1,0:T(8,128)} copy(f32[1024,1024]{1,0:T(8,128)S(1)} %copy-done) | data formatting | bytes 8388608
  (2 shorter events, 0.0 us)
Async XLA Ops:
  6.5 36.3 %all-to-all-start.1 = ((f32[512,32,32]{0,2,1:T(8,128)}), f32[512,32,32]{0,2,1:T(8,128)S(1)}, u32[]{:S(2)}, u32[]{:S(2)}) async-start(f32[512,32,32]{0,2,1:T(8,128)} %bitcast.8), calls=%async_computation.1 | async-start | bytes 4194304 | tf_op jit(solution)/shard_map/all_to_all | solution.py:225
  42.8 4.9 %copy-start.1 = (s32[32,2]{0,1:T(2,128)S(1)}, s32[32,2]{0,1:T(2,128)}, u32[]{:S(2)}) copy-start(s32[32,2]{0,1:T(2,128)} %param.3) | copy-start | bytes 772
  42.8 33.8 %all-to-all-start = ((f32[512,32,32]{0,2,1:T(8,128)}), f32[512,32,32]{0,2,1:T(8,128)}, u32[]{:S(2)}, u32[]{:S(2)}) async-start(f32[512,32,32]{0,2,1:T(8,128)} %bitcast.7), calls=%async_computation | async-start | bytes 4194304 | tf_op jit(solution)/shard_map/all_to_all | solution.py:225
  152.9 5.0 %copy-start = (f32[1024,1024]{1,0:T(8,128)S(1)}, f32[1024,1024]{1,0:T(8,128)}, u32[]{:S(2)}) copy-start(f32[1024,1024]{1,0:T(8,128)} %get-tuple-element.7) | copy-start | bytes 12582916

commit v6 on v4

--- a/solution.py
+++ b/solution.py
@@ -30,7 +30,8 @@
 
 def inspect_kernel(
     band_rows, band_cols, prm, tile, diff_out, defect_out,
-    s0, s1, s2, s3, fv_last, held, from_left, from_right, send_sem, recv_sem, halo_send, halo_recv,
+    s0, s1, s2, s3, fv_last, held, from_left, from_right, send_sem, recv_sem, halo_send, halo_recv, load_sem,
+    defect_buf, out_sem,
 ):
     rows, width = tile.shape
     ext_w = s0.shape[1]
@@ -78,6 +79,8 @@
             device_id_type=mesh_ids,
         )
 
+    load = pltpu.make_async_copy(tile, s0.at[mid_rows, all_cols], load_sem.at[0])
+    load.start()
     barrier = pltpu.get_barrier_semaphore()
     for target, _, _ in halo_plan:
         pl.semaphore_signal(barrier, inc=1, device_id=target, device_id_type=mesh_ids)
@@ -90,7 +93,7 @@
         buf[pl.ds(0, PAD), :] = zeros_pad
         buf[pl.ds(PAD + ext_r, PAD), :] = zeros_pad
     fv_last[...] = jnp.zeros(fv_last.shape, jnp.float32)
-    s0[mid_rows, all_cols] = tile[...]
+    load.wait()
     for n in range(len(halo_plan)):
         halo_copy(n).wait_recv()
     for n in range(len(halo_plan)):
@@ -165,7 +168,8 @@
         return carry
 
     lax.fori_loop(0, blocks + STEPS, wave, 0)
-    diff_out[...] = s0[pl.ds(PAD + ROWH, rows), pl.ds(0, width)]
+    diff_copy = pltpu.make_async_copy(s0.at[mid_rows, all_cols], diff_out, out_sem.at[0])
+    diff_copy.start()
 
     def finish(a, carry):
         for side_index in (0, 1):
@@ -173,10 +177,14 @@
         for side_index in (0, 1):
             send(a, side_index).wait_send()
         rows_a = pl.ds(pl.multiple_of(a * BLK, BLK), BLK)
-        defect_out[rows_a, :] = three_die(held[rows_a, :], from_left[rows_a, :], from_right[rows_a, :])
+        defect_buf[rows_a, :] = three_die(held[rows_a, :], from_left[rows_a, :], from_right[rows_a, :])
         return carry
 
     lax.fori_loop(0, out_blocks, finish, 0)
+    defect_copy = pltpu.make_async_copy(defect_buf, defect_out, out_sem.at[1])
+    defect_copy.start()
+    diff_copy.wait()
+    defect_copy.wait()
 
 
 def inspect(prm, tile, band_rows, band_cols):
@@ -185,12 +193,11 @@
     out_blocks = rows // BLK
     buf = pltpu.VMEM((rows + 2 * ROWH + 2 * PAD, ext_w), jnp.float32)
     die = pltpu.VMEM((rows, width), jnp.float32)
-    vspec = pl.BlockSpec(memory_space=pltpu.VMEM)
     return pl.pallas_call(
         functools.partial(inspect_kernel, band_rows, band_cols),
         out_shape=(jax.ShapeDtypeStruct((rows, width), jnp.float32),) * 2,
-        in_specs=[pl.BlockSpec(memory_space=pltpu.SMEM), vspec],
-        out_specs=(vspec, vspec),
+        in_specs=[pl.BlockSpec(memory_space=pltpu.SMEM), pl.BlockSpec(memory_space=pl.ANY)],
+        out_specs=(pl.BlockSpec(memory_space=pl.ANY), pl.BlockSpec(memory_space=pl.ANY)),
         scratch_shapes=[
             buf, buf, buf, buf,
             pltpu.VMEM((STEPS, 8, ext_w), jnp.float32),
@@ -199,6 +206,9 @@
             pltpu.SemaphoreType.DMA((2, out_blocks)),
             pltpu.SemaphoreType.DMA((8,)),
             pltpu.SemaphoreType.DMA((8,)),
+            pltpu.SemaphoreType.DMA((1,)),
+            die,
+            pltpu.SemaphoreType.DMA((2,)),
         ],
         compiler_params=pltpu.CompilerParams(
             vmem_limit_bytes=64000 * 1024, collective_id=0, has_side_effects=True

time: 153 us -> 151 us (0.987)
  Pallas kernels: 73.7 us -> 71.2 us
    pallas_call x1, Pallas kernels: 73.7 us -> 71.2 us  [inspect(): pl.pallas_call(functools.partial(inspect_kernel, band_rows, band_cols), o...]
where the time goes in v6:
time: 151 us; the launch traced here: 150 us
  Pallas kernels  71.2 us (47%)
  waiting for transfers between devices  52 us (34%)
  local copies, waits for them, and re-layouts  17.6 us (12%)
  starting transfers between devices  7.67 us (5%)
    pallas_call x1, Pallas kernels, inspect(): pl.pallas_call(functools.partial(inspect_kernel, band_rows, band_cols), o...  71.2 us
    all_to_all x1, waiting for transfers between devices, local(): lax.all_to_all(raw_band, 'col', split_axis=1, concat_axis=1, tiled=True)  52 us
    unnamed x7, local copies, waits for them, and re-layouts  12.3 us
    all_to_all x1, starting transfers between devices, local(): lax.all_to_all(raw_band, 'col', split_axis=1, concat_axis=1, tiled=True)  7.67 us
    all_to_all x1, local copies, waits for them, and re-layouts, local(): lax.all_to_all(raw_band, 'col', split_axis=1, concat_axis=1, tiled=True)  5.34 us
  transfers between devices with their start and end apart: 1, of which 1 were waited for; matrix products, arithmetic and copies ran while one was open for 0% of the time, Pallas kernels for 0%

profile of v6, /device:TPU:0, one launch (start us, length us, event | category | flops | bytes accessed | tf_op | source)
XLA Modules:
  0.0 149.9 jit_solution(14530517464470347481)
XLA Ops:
  0.6 5.3 %copy.4 = f32[1024,1024]{0,1:T(8,128)} copy(f32[1024,1024]{1,0:T(8,128)} %param.2) | data formatting | bytes 8388608 | tf_op args[0]
  6.0 0.0 copy-start.1
  6.0 7.7 %all-to-all-start = ((f32[1024,32,32]{0,2,1:T(8,128)}), f32[1024,32,32]{0,2,1:T(8,128)}, u32[]{:S(2)}, u32[]{:S(2)}) async-start(f32[1024,32,32]{0,2,1:T(8,128)} %bitcast.4), calls=%async_computation | async-start | bytes 8388608 | tf_op jit(solution)/shard_map/all_to_all | solution.py:226
  13.7 0.0 copy-done.1
  13.7 0.1 select_reduce_fusion
  13.8 0.6 pad_add_fusion.prm
  14.4 52.0 %all-to-all-done = f32[1024,32,32]{0,2,1:T(8,128)} async-done(((f32[1024,32,32]{0,2,1:T(8,128)}), f32[1024,32,32]{0,2,1:T(8,128)}, u32[]{:S(2)}, u32[]{:S(2)}) %all-to-all-start) | async-done | bytes 4194336 | tf_op jit(solution)/shard_map/all_to_all | solution.py:226
  66.4 5.3 %copy.5.tile = f32[1024,1024]{1,0:T(8,128)} copy(f32[1024,1024]{0,1:T(8,128)} %bitcast.3) | data formatting | bytes 8388608 | tf_op jit(solution)/shard_map/all_to_all | solution.py:226
  71.8 71.2 %shard_map.41 = (f32[1024,1024]{1,0:T(8,128)}, f32[1024,1024]{1,0:T(8,128)}) custom-call(s32[8]{0:T(128)} %pad_add_fusion.prm, f32[1024,1024]{1,0:T(8,128)} %copy.5.tile), custom_call_target="tpu_custom_call" | custom-call | flops 222822400 | bytes 12582912 | tf_op jit(solution)/shard_map/pallas_call | solution.py:196
  143.0 0.0 copy-start
  143.0 4.9 %copy.8 = f32[1024,1024]{1,0:T(8,128)} copy(f32[1024,1024]{1,0:T(8,128)} %get-tuple-element.4) | data formatting | bytes 8388608
  147.9 0.0 copy-done
  147.9 2.0 %copy.9 = f32[1024,1024]{1,0:T(8,128)} copy(f32[1024,1024]{1,0:T(8,128)S(1)} %copy-done) | data formatting | bytes 8388608
  (2 shorter events, 0.0 us)
Async XLA Ops:
  6.0 7.7 %copy-start.1 = (s32[32,2]{0,1:T(2,128)S(1)}, s32[32,2]{0,1:T(2,128)}, u32[]{:S(2)}) copy-start(s32[32,2]{0,1:T(2,128)} %param.3) | copy-start | bytes 772
  6.0 60.5 %all-to-all-start = ((f32[1024,32,32]{0,2,1:T(8,128)}), f32[1024,32,32]{0,2,1:T(8,128)}, u32[]{:S(2)}, u32[]{:S(2)}) async-start(f32[1024,32,32]{0,2,1:T(8,128)} %bitcast.4), calls=%async_computation | async-start | bytes 8388608 | tf_op jit(solution)/shard_map/all_to_all | solution.py:226
  143.0 5.0 %copy-start = (f32[1024,1024]{1,0:T(8,128)S(1)}, f32[1024,1024]{1,0:T(8,128)}, u32[]{:S(2)}) copy-start(f32[1024,1024]{1,0:T(8,128)} %get-tuple-element.5) | copy-start | bytes 12582916

commit v7 on v6

--- a/solution.py
+++ b/solution.py
@@ -29,11 +29,11 @@
 
 
 def inspect_kernel(
-    band_rows, band_cols, prm, tile, diff_out, defect_out,
+    band_rows, band_cols, prm, raw_t, diff_out, defect_out,
     s0, s1, s2, s3, fv_last, held, from_left, from_right, send_sem, recv_sem, halo_send, halo_recv, load_sem,
-    defect_buf, out_sem,
+    defect_buf, out_sem, tile_t,
 ):
-    rows, width = tile.shape
+    width, rows = raw_t.shape
     ext_w = s0.shape[1]
     ext_r = rows + 2 * ROWH
     blocks = ext_r // BLK
@@ -70,8 +70,9 @@
 
     def halo_copy(n):
         target, src, dst = halo_plan[n]
+        rows_src, cols_src = src
         return pltpu.make_async_remote_copy(
-            src_ref=tile.at[src],
+            src_ref=s0.at[pl.ds(PAD + ROWH + rows_src.start, rows_src.size), cols_src],
             dst_ref=s0.at[dst],
             send_sem=halo_send.at[n],
             recv_sem=halo_recv.at[n],
@@ -79,12 +80,21 @@
             device_id_type=mesh_ids,
         )
 
-    load = pltpu.make_async_copy(tile, s0.at[mid_rows, all_cols], load_sem.at[0])
+    load = pltpu.make_async_copy(raw_t, tile_t, load_sem.at[0])
     load.start()
     barrier = pltpu.get_barrier_semaphore()
     for target, _, _ in halo_plan:
         pl.semaphore_signal(barrier, inc=1, device_id=target, device_id_type=mesh_ids)
     pl.semaphore_wait(barrier, len(halo_plan))
+    load.wait()
+
+    def flip_rows(i, carry):
+        for j in range(width // 128):
+            block = tile_t[pl.ds(j * 128, 128), pl.ds(pl.multiple_of(i * 128, 128), 128)]
+            s0[pl.ds(pl.multiple_of(PAD + ROWH + i * 128, 8), 128), pl.ds(j * 128, 128)] = block.T
+        return carry
+
+    lax.fori_loop(0, rows // 128, flip_rows, 0)
     for n in range(len(halo_plan)):
         halo_copy(n).start()
 
@@ -93,7 +103,6 @@
         buf[pl.ds(0, PAD), :] = zeros_pad
         buf[pl.ds(PAD + ext_r, PAD), :] = zeros_pad
     fv_last[...] = jnp.zeros(fv_last.shape, jnp.float32)
-    load.wait()
     for n in range(len(halo_plan)):
         halo_copy(n).wait_recv()
     for n in range(len(halo_plan)):
@@ -187,8 +196,8 @@
     defect_copy.wait()
 
 
-def inspect(prm, tile, band_rows, band_cols):
-    rows, width = tile.shape
+def inspect(prm, raw_t, band_rows, band_cols):
+    width, rows = raw_t.shape
     ext_w = width + 2 * COLH
     out_blocks = rows // BLK
     buf = pltpu.VMEM((rows + 2 * ROWH + 2 * PAD, ext_w), jnp.float32)
@@ -209,6 +218,7 @@
             pltpu.SemaphoreType.DMA((1,)),
             die,
             pltpu.SemaphoreType.DMA((2,)),
+            die,
         ],
         compiler_params=pltpu.CompilerParams(
             vmem_limit_bytes=64000 * 1024, collective_id=0, has_side_effects=True
@@ -216,14 +226,14 @@
         cost_estimate=pl.CostEstimate(
             flops=STEPS * 40 * (rows + 2 * ROWH) * ext_w, bytes_accessed=4 * 3 * rows * width, transcendentals=0
         ),
-    )(prm, tile)
+    )(prm, raw_t)
 
 
 def local(raw_band, section_offsets):
     col_count = lax.axis_size("col")
     swath_count = lax.axis_size("swath")
     row_total, die_width = raw_band.shape
-    die_tile = lax.all_to_all(raw_band, "col", split_axis=1, concat_axis=1, tiled=True)
+    raw_t = lax.all_to_all(raw_band.T, "col", split_axis=0, concat_axis=0, tiled=True)
     swath_index = lax.axis_index("swath")
     col_index = lax.axis_index("col")
     band_rows = swath_count * row_total
@@ -234,7 +244,7 @@
         [swath_index * row_total, col_index * die_width, own_shift[0], own_shift[1]]
         + [jnp.int32(0)] * 4
     ).astype(jnp.int32)
-    return inspect(prm, die_tile, band_rows, band_cols)
+    return inspect(prm, raw_t, band_rows, band_cols)
 
 
 def solution(mesh):

time: 151 us -> 147 us (0.974)
  local copies, waits for them, and re-layouts: 17.6 us -> 12.3 us
  Pallas kernels: 71.2 us -> 73.6 us
    all_to_all x1 -> x0, local copies, waits for them, and re-layouts: 5.34 us -> none  [local(): lax.all_to_all(raw_band, 'col', split_axis=1, concat_axis=1, tiled=True)]
    pallas_call x1, Pallas kernels: 71.2 us -> 73.6 us  [inspect(): pl.pallas_call(functools.partial(inspect_kernel, band_rows, band_cols), o...]
  transfers between devices with their start and end apart: 1 -> 1, of which waited for: 1 -> 1; matrix products, arithmetic and copies ran while one was open for 0% -> 1% of each run, Pallas kernels for 0% -> 0%
where the time goes in v7:
time: 147 us
  Pallas kernels  73.6 us (50%)
  waiting for transfers between devices  52 us (35%)
  local copies, waits for them, and re-layouts  12.3 us (8%)
  starting transfers between devices  7.67 us (5%)
    pallas_call x1, Pallas kernels, inspect(): pl.pallas_call(functools.partial(inspect_kernel, band_rows, band_cols), o...  73.6 us
    all_to_all x1, waiting for transfers between devices, local(): lax.all_to_all(raw_band.T, 'col', split_axis=0, concat_axis=0, tiled=True)  52 us
    unnamed x7, local copies, waits for them, and re-layouts  12.3 us
    all_to_all x1, starting transfers between devices, local(): lax.all_to_all(raw_band.T, 'col', split_axis=0, concat_axis=0, tiled=True)  7.67 us
  transfers between devices with their start and end apart: 1, of which 1 were waited for; matrix products, arithmetic and copies ran while one was open for 1% of the time, Pallas kernels for 0%

profile of v7, /device:TPU:0, one launch (start us, length us, event | category | flops | bytes accessed | tf_op | source)
XLA Modules:
  0.0 147.0 jit_solution(1706197443174177448)
XLA Ops:
  0.6 5.3 %copy.5 = f32[1024,1024]{0,1:T(8,128)} copy(f32[1024,1024]{1,0:T(8,128)} %param.2) | data formatting | bytes 8388608 | tf_op args[0]
  6.0 0.0 copy-start.1
  6.0 7.7 %all-to-all-start = ((f32[32,32,1024]{2,1,0:T(8,128)}), f32[32,32,1024]{2,1,0:T(8,128)}, u32[]{:S(2)}, u32[]{:S(2)}) async-start(f32[32,32,1024]{2,1,0:T(8,128)} %bitcast.6), calls=%async_computation | async-start | bytes 8388608 | tf_op jit(solution)/shard_map/all_to_all | solution.py:236
  13.7 0.0 copy-done.1
  13.7 0.1 select_reduce_fusion
  13.8 0.7 pad_add_fusion.prm
  14.5 52.0 %all-to-all-done = f32[32,32,1024]{2,1,0:T(8,128)} async-done(((f32[32,32,1024]{2,1,0:T(8,128)}), f32[32,32,1024]{2,1,0:T(8,128)}, u32[]{:S(2)}, u32[]{:S(2)}) %all-to-all-start) | async-done | bytes 4194336 | tf_op jit(solution)/shard_map/all_to_all | solution.py:236
  66.4 73.6 %shard_map.41 = (f32[1024,1024]{1,0:T(8,128)}, f32[1024,1024]{1,0:T(8,128)}) custom-call(s32[8]{0:T(128)} %pad_add_fusion.prm, f32[1024,1024]{1,0:T(8,128)} %bitcast.4.raw_t), custom_call_target="tpu_custom_call" | custom-call | flops 222822400 | bytes 12582912 | tf_op jit(solution)/shard_map/pallas_call | solution.py:205
  140.0 0.0 copy-start
  140.1 4.9 %copy.8 = f32[1024,1024]{1,0:T(8,128)} copy(f32[1024,1024]{1,0:T(8,128)} %get-tuple-element.4) | data formatting | bytes 8388608
  145.0 0.0 copy-done
  145.0 2.0 %copy.9 = f32[1024,1024]{1,0:T(8,128)} copy(f32[1024,1024]{1,0:T(8,128)S(1)} %copy-done) | data formatting | bytes 8388608
  (2 shorter events, 0.0 us)
Async XLA Ops:
  6.0 7.7 %copy-start.1 = (s32[32,2]{0,1:T(2,128)S(1)}, s32[32,2]{0,1:T(2,128)}, u32[]{:S(2)}) copy-start(s32[32,2]{0,1:T(2,128)} %param.3) | copy-start | bytes 772
  6.0 60.5 %all-to-all-start = ((f32[32,32,1024]{2,1,0:T(8,128)}), f32[32,32,1024]{2,1,0:T(8,128)}, u32[]{:S(2)}, u32[]{:S(2)}) async-start(f32[32,32,1024]{2,1,0:T(8,128)} %bitcast.6), calls=%async_computation | async-start | bytes 8388608 | tf_op jit(solution)/shard_map/all_to_all | solution.py:236
  140.0 5.0 %copy-start = (f32[1024,1024]{1,0:T(8,128)S(1)}, f32[1024,1024]{1,0:T(8,128)}, u32[]{:S(2)}) copy-start(f32[1024,1024]{1,0:T(8,128)} %get-tuple-element.5) | copy-start | bytes 12582916

commit v8 on v7

--- a/solution.py
+++ b/solution.py
@@ -80,21 +80,26 @@
             device_id_type=mesh_ids,
         )
 
-    load = pltpu.make_async_copy(raw_t, tile_t, load_sem.at[0])
-    load.start()
+    strips = [
+        pltpu.make_async_copy(raw_t.at[pl.ds(j * 128, 128)], tile_t.at[pl.ds(j * 128, 128)], load_sem.at[j])
+        for j in range(width // 128)
+    ]
+    for strip in strips:
+        strip.start()
     barrier = pltpu.get_barrier_semaphore()
     for target, _, _ in halo_plan:
         pl.semaphore_signal(barrier, inc=1, device_id=target, device_id_type=mesh_ids)
     pl.semaphore_wait(barrier, len(halo_plan))
-    load.wait()
-
-    def flip_rows(i, carry):
-        for j in range(width // 128):
+
+    for j, strip in enumerate(strips):
+        strip.wait()
+
+        def flip_strip(i, carry, j=j):
             block = tile_t[pl.ds(j * 128, 128), pl.ds(pl.multiple_of(i * 128, 128), 128)]
             s0[pl.ds(pl.multiple_of(PAD + ROWH + i * 128, 8), 128), pl.ds(j * 128, 128)] = block.T
-        return carry
-
-    lax.fori_loop(0, rows // 128, flip_rows, 0)
+            return carry
+
+        lax.fori_loop(0, rows // 128, flip_strip, 0)
     for n in range(len(halo_plan)):
         halo_copy(n).start()
 
@@ -187,11 +192,11 @@
             send(a, side_index).wait_send()
         rows_a = pl.ds(pl.multiple_of(a * BLK, BLK), BLK)
         defect_buf[rows_a, :] = three_die(held[rows_a, :], from_left[rows_a, :], from_right[rows_a, :])
+        pltpu.make_async_copy(defect_buf.at[rows_a], defect_out.at[rows_a], out_sem.at[1]).start()
         return carry
 
     lax.fori_loop(0, out_blocks, finish, 0)
     defect_copy = pltpu.make_async_copy(defect_buf, defect_out, out_sem.at[1])
-    defect_copy.start()
     diff_copy.wait()
     defect_copy.wait()
 
@@ -215,7 +220,7 @@
             pltpu.SemaphoreType.DMA((2, out_blocks)),
             pltpu.SemaphoreType.DMA((8,)),
             pltpu.SemaphoreType.DMA((8,)),
-            pltpu.SemaphoreType.DMA((1,)),
+            pltpu.SemaphoreType.DMA((width // 128,)),
             die,
             pltpu.SemaphoreType.DMA((2,)),
             die,

time: 147 us -> 150 us (1.020)
  Pallas kernels: 73.6 us -> 76.1 us
    pallas_call x1, Pallas kernels: 73.6 us -> 76.1 us  [inspect(): pl.pallas_call(functools.partial(inspect_kernel, band_rows, band_cols), o...]
where the time goes in v8:
time: 150 us
  Pallas kernels  76.1 us (51%)
  waiting for transfers between devices  52 us (35%)
  local copies, waits for them, and re-layouts  12.3 us (8%)
  starting transfers between devices  7.67 us (5%)
    pallas_call x1, Pallas kernels, inspect(): pl.pallas_call(functools.partial(inspect_kernel, band_rows, band_cols), o...  76.1 us
    all_to_all x1, waiting for transfers between devices, local(): lax.all_to_all(raw_band.T, 'col', split_axis=0, concat_axis=0, tiled=True)  52 us
    unnamed x7, local copies, waits for them, and re-layouts  12.3 us
    all_to_all x1, starting transfers between devices, local(): lax.all_to_all(raw_band.T, 'col', split_axis=0, concat_axis=0, tiled=True)  7.67 us
  transfers between devices with their start and end apart: 1, of which 1 were waited for; matrix products, arithmetic and copies ran while one was open for 1% of the time, Pallas kernels for 0%

profile of v8, /device:TPU:0, one launch (start us, length us, event | category | flops | bytes accessed | tf_op | source)
XLA Modules:
  0.0 149.5 jit_solution(8837355669307543381)
XLA Ops:
  0.6 5.3 %copy.5 = f32[1024,1024]{0,1:T(8,128)} copy(f32[1024,1024]{1,0:T(8,128)} %param.2) | data formatting | bytes 8388608 | tf_op args[0]
  6.0 0.0 copy-start.1
  6.0 7.7 %all-to-all-start = ((f32[32,32,1024]{2,1,0:T(8,128)}), f32[32,32,1024]{2,1,0:T(8,128)}, u32[]{:S(2)}, u32[]{:S(2)}) async-start(f32[32,32,1024]{2,1,0:T(8,128)} %bitcast.6), calls=%async_computation | async-start | bytes 8388608 | tf_op jit(solution)/shard_map/all_to_all | solution.py:241
  13.7 0.0 copy-done.1
  13.7 0.1 select_reduce_fusion
  13.8 0.7 pad_add_fusion.prm
  14.5 52.0 %all-to-all-done = f32[32,32,1024]{2,1,0:T(8,128)} async-done(((f32[32,32,1024]{2,1,0:T(8,128)}), f32[32,32,1024]{2,1,0:T(8,128)}, u32[]{:S(2)}, u32[]{:S(2)}) %all-to-all-start) | async-done | bytes 4194336 | tf_op jit(solution)/shard_map/all_to_all | solution.py:241
  66.4 76.1 %shard_map.41 = (f32[1024,1024]{1,0:T(8,128)}, f32[1024,1024]{1,0:T(8,128)}) custom-call(s32[8]{0:T(128)} %pad_add_fusion.prm, f32[1024,1024]{1,0:T(8,128)} %bitcast.4.raw_t), custom_call_target="tpu_custom_call" | custom-call | flops 222822400 | bytes 12582912 | tf_op jit(solution)/shard_map/pallas_call | solution.py:210
  142.6 0.0 copy-start
  142.6 4.9 %copy.8 = f32[1024,1024]{1,0:T(8,128)} copy(f32[1024,1024]{1,0:T(8,128)} %get-tuple-element.4) | data formatting | bytes 8388608
  147.5 0.0 copy-done
  147.5 2.0 %copy.9 = f32[1024,1024]{1,0:T(8,128)} copy(f32[1024,1024]{1,0:T(8,128)S(1)} %copy-done) | data formatting | bytes 8388608
  (2 shorter events, 0.0 us)
Async XLA Ops:
  6.0 7.7 %copy-start.1 = (s32[32,2]{0,1:T(2,128)S(1)}, s32[32,2]{0,1:T(2,128)}, u32[]{:S(2)}) copy-start(s32[32,2]{0,1:T(2,128)} %param.3) | copy-start | bytes 772
  6.0 60.5 %all-to-all-start = ((f32[32,32,1024]{2,1,0:T(8,128)}), f32[32,32,1024]{2,1,0:T(8,128)}, u32[]{:S(2)}, u32[]{:S(2)}) async-start(f32[32,32,1024]{2,1,0:T(8,128)} %bitcast.6), calls=%async_computation | async-start | bytes 8388608 | tf_op jit(solution)/shard_map/all_to_all | solution.py:241
  142.6 5.0 %copy-start = (f32[1024,1024]{1,0:T(8,128)S(1)}, f32[1024,1024]{1,0:T(8,128)}, u32[]{:S(2)}) copy-start(f32[1024,1024]{1,0:T(8,128)} %get-tuple-element.5) | copy-start | bytes 12582916

commit v9 on v7

--- a/solution.py
+++ b/solution.py
@@ -187,11 +187,11 @@
             send(a, side_index).wait_send()
         rows_a = pl.ds(pl.multiple_of(a * BLK, BLK), BLK)
         defect_buf[rows_a, :] = three_die(held[rows_a, :], from_left[rows_a, :], from_right[rows_a, :])
+        pltpu.make_async_copy(defect_buf.at[rows_a], defect_out.at[rows_a], out_sem.at[1]).start()
         return carry
 
     lax.fori_loop(0, out_blocks, finish, 0)
     defect_copy = pltpu.make_async_copy(defect_buf, defect_out, out_sem.at[1])
-    defect_copy.start()
     diff_copy.wait()
     defect_copy.wait()
 

time: 147 us -> 146 us (level)
  no operation moved by 1% of the time
where the time goes in v9:
time: 146 us
  Pallas kernels  72.3 us (50%)
  waiting for transfers between devices  52 us (36%)
  local copies, waits for them, and re-layouts  12.3 us (8%)
  starting transfers between devices  7.67 us (5%)
    pallas_call x1, Pallas kernels, inspect(): pl.pallas_call(functools.partial(inspect_kernel, band_rows, band_cols), o...  72.3 us
    all_to_all x1, waiting for transfers between devices, local(): lax.all_to_all(raw_band.T, 'col', split_axis=0, concat_axis=0, tiled=True)  52 us
    unnamed x7, local copies, waits for them, and re-layouts  12.3 us
    all_to_all x1, starting transfers between devices, local(): lax.all_to_all(raw_band.T, 'col', split_axis=0, concat_axis=0, tiled=True)  7.67 us
  transfers between devices with their start and end apart: 1, of which 1 were waited for; matrix products, arithmetic and copies ran while one was open for 1% of the time, Pallas kernels for 0%

profile of v9, /device:TPU:0, one launch (start us, length us, event | category | flops | bytes accessed | tf_op | source)
XLA Modules:
  0.0 145.8 jit_solution(11703736148524469729)
XLA Ops:
  0.6 5.3 %copy.5 = f32[1024,1024]{0,1:T(8,128)} copy(f32[1024,1024]{1,0:T(8,128)} %param.2) | data formatting | bytes 8388608 | tf_op args[0]
  6.0 0.0 copy-start.1
  6.0 7.7 %all-to-all-start = ((f32[32,32,1024]{2,1,0:T(8,128)}), f32[32,32,1024]{2,1,0:T(8,128)}, u32[]{:S(2)}, u32[]{:S(2)}) async-start(f32[32,32,1024]{2,1,0:T(8,128)} %bitcast.6), calls=%async_computation | async-start | bytes 8388608 | tf_op jit(solution)/shard_map/all_to_all | solution.py:236
  13.7 0.0 copy-done.1
  13.7 0.1 select_reduce_fusion
  13.8 0.7 pad_add_fusion.prm
  14.5 52.0 %all-to-all-done = f32[32,32,1024]{2,1,0:T(8,128)} async-done(((f32[32,32,1024]{2,1,0:T(8,128)}), f32[32,32,1024]{2,1,0:T(8,128)}, u32[]{:S(2)}, u32[]{:S(2)}) %all-to-all-start) | async-done | bytes 4194336 | tf_op jit(solution)/shard_map/all_to_all | solution.py:236
  66.4 72.3 %shard_map.41 = (f32[1024,1024]{1,0:T(8,128)}, f32[1024,1024]{1,0:T(8,128)}) custom-call(s32[8]{0:T(128)} %pad_add_fusion.prm, f32[1024,1024]{1,0:T(8,128)} %bitcast.4.raw_t), custom_call_target="tpu_custom_call" | custom-call | flops 222822400 | bytes 12582912 | tf_op jit(solution)/shard_map/pallas_call | solution.py:205
  138.8 0.0 copy-start
  138.8 4.9 %copy.8 = f32[1024,1024]{1,0:T(8,128)} copy(f32[1024,1024]{1,0:T(8,128)} %get-tuple-element.4) | data formatting | bytes 8388608
  143.7 0.0 copy-done
  143.7 2.0 %copy.9 = f32[1024,1024]{1,0:T(8,128)} copy(f32[1024,1024]{1,0:T(8,128)S(1)} %copy-done) | data formatting | bytes 8388608
  (2 shorter events, 0.0 us)
Async XLA Ops:
  6.0 7.7 %copy-start.1 = (s32[32,2]{0,1:T(2,128)S(1)}, s32[32,2]{0,1:T(2,128)}, u32[]{:S(2)}) copy-start(s32[32,2]{0,1:T(2,128)} %param.3) | copy-start | bytes 772
  6.0 60.5 %all-to-all-start = ((f32[32,32,1024]{2,1,0:T(8,128)}), f32[32,32,1024]{2,1,0:T(8,128)}, u32[]{:S(2)}, u32[]{:S(2)}) async-start(f32[32,32,1024]{2,1,0:T(8,128)} %bitcast.6), calls=%async_computation | async-start | bytes 8388608 | tf_op jit(solution)/shard_map/all_to_all | solution.py:236
  138.8 5.0 %copy-start = (f32[1024,1024]{1,0:T(8,128)S(1)}, f32[1024,1024]{1,0:T(8,128)}, u32[]{:S(2)}) copy-start(f32[1024,1024]{1,0:T(8,128)} %get-tuple-element.5) | copy-start | bytes 12582916

commit v10 on v9

--- a/solution.py
+++ b/solution.py
@@ -88,15 +88,24 @@
     pl.semaphore_wait(barrier, len(halo_plan))
     load.wait()
 
-    def flip_rows(i, carry):
-        for j in range(width // 128):
-            block = tile_t[pl.ds(j * 128, 128), pl.ds(pl.multiple_of(i * 128, 128), 128)]
-            s0[pl.ds(pl.multiple_of(PAD + ROWH + i * 128, 8), 128), pl.ds(j * 128, 128)] = block.T
-        return carry
-
-    lax.fori_loop(0, rows // 128, flip_rows, 0)
+    def flip(i, j):
+        block = tile_t[pl.ds(j * 128, 128), pl.ds(pl.multiple_of(i * 128, 128), 128)]
+        s0[pl.ds(pl.multiple_of(PAD + ROWH + i * 128, 8), 128), pl.ds(j * 128, 128)] = block.T
+
+    row_bands, col_bands = rows // 128, width // 128
+    for i in range(row_bands):
+        for j in range(col_bands):
+            if i in (0, row_bands - 1) or j in (0, col_bands - 1):
+                flip(i, j)
     for n in range(len(halo_plan)):
         halo_copy(n).start()
+
+    def flip_inner(i, carry):
+        for j in range(1, col_bands - 1):
+            flip(i, j)
+        return carry
+
+    lax.fori_loop(1, row_bands - 1, flip_inner, 0)
 
     zeros_pad = jnp.zeros((PAD, ext_w), jnp.float32)
     for buf in (s0, s1, s2, s3):

time: 146 us -> 145 us (level)
  no operation moved by 1% of the time
where the time goes in v10:
time: 145 us
  Pallas kernels  71.3 us (49%)
  waiting for transfers between devices  52 us (36%)
  local copies, waits for them, and re-layouts  12.3 us (8%)
  starting transfers between devices  7.67 us (5%)
    pallas_call x1, Pallas kernels, inspect(): pl.pallas_call(functools.partial(inspect_kernel, band_rows, band_cols), o...  71.3 us
    all_to_all x1, waiting for transfers between devices, local(): lax.all_to_all(raw_band.T, 'col', split_axis=0, concat_axis=0, tiled=True)  52 us
    unnamed x7, local copies, waits for them, and re-layouts  12.3 us
    all_to_all x1, starting transfers between devices, local(): lax.all_to_all(raw_band.T, 'col', split_axis=0, concat_axis=0, tiled=True)  7.67 us
  transfers between devices with their start and end apart: 1, of which 1 were waited for; matrix products, arithmetic and copies ran while one was open for 1% of the time, Pallas kernels for 0%

profile of v10, /device:TPU:0, one launch (start us, length us, event | category | flops | bytes accessed | tf_op | source)
XLA Modules:
  0.0 144.7 jit_solution(12432395914326314669)
XLA Ops:
  0.6 5.3 %copy.5 = f32[1024,1024]{0,1:T(8,128)} copy(f32[1024,1024]{1,0:T(8,128)} %param.2) | data formatting | bytes 8388608 | tf_op args[0]
  6.0 0.0 copy-start.1
  6.0 7.7 %all-to-all-start = ((f32[32,32,1024]{2,1,0:T(8,128)}), f32[32,32,1024]{2,1,0:T(8,128)}, u32[]{:S(2)}, u32[]{:S(2)}) async-start(f32[32,32,1024]{2,1,0:T(8,128)} %bitcast.6), calls=%async_computation | async-start | bytes 8388608 | tf_op jit(solution)/shard_map/all_to_all | solution.py:245
  13.7 0.0 copy-done.1
  13.7 0.1 select_reduce_fusion
  13.8 0.7 pad_add_fusion.prm
  14.5 52.0 %all-to-all-done = f32[32,32,1024]{2,1,0:T(8,128)} async-done(((f32[32,32,1024]{2,1,0:T(8,128)}), f32[32,32,1024]{2,1,0:T(8,128)}, u32[]{:S(2)}, u32[]{:S(2)}) %all-to-all-start) | async-done | bytes 4194336 | tf_op jit(solution)/shard_map/all_to_all | solution.py:245
  66.4 71.3 %shard_map.41 = (f32[1024,1024]{1,0:T(8,128)}, f32[1024,1024]{1,0:T(8,128)}) custom-call(s32[8]{0:T(128)} %pad_add_fusion.prm, f32[1024,1024]{1,0:T(8,128)} %bitcast.4.raw_t), custom_call_target="tpu_custom_call" | custom-call | flops 222822400 | bytes 12582912 | tf_op jit(solution)/shard_map/pallas_call | solution.py:214
  137.7 0.0 copy-start
  137.7 4.9 %copy.8 = f32[1024,1024]{1,0:T(8,128)} copy(f32[1024,1024]{1,0:T(8,128)} %get-tuple-element.4) | data formatting | bytes 8388608
  142.7 0.0 copy-done
  142.7 2.0 %copy.9 = f32[1024,1024]{1,0:T(8,128)} copy(f32[1024,1024]{1,0:T(8,128)S(1)} %copy-done) | data formatting | bytes 8388608
  (2 shorter events, 0.0 us)
Async XLA Ops:
  6.0 7.7 %copy-start.1 = (s32[32,2]{0,1:T(2,128)S(1)}, s32[32,2]{0,1:T(2,128)}, u32[]{:S(2)}) copy-start(s32[32,2]{0,1:T(2,128)} %param.3) | copy-start | bytes 772
  6.0 60.5 %all-to-all-start = ((f32[32,32,1024]{2,1,0:T(8,128)}), f32[32,32,1024]{2,1,0:T(8,128)}, u32[]{:S(2)}, u32[]{:S(2)}) async-start(f32[32,32,1024]{2,1,0:T(8,128)} %bitcast.6), calls=%async_computation | async-start | bytes 8388608 | tf_op jit(solution)/shard_map/all_to_all | solution.py:245
  137.7 5.0 %copy-start = (f32[1024,1024]{1,0:T(8,128)S(1)}, f32[1024,1024]{1,0:T(8,128)}, u32[]{:S(2)}) copy-start(f32[1024,1024]{1,0:T(8,128)} %get-tuple-element.5) | copy-start | bytes 12582916

commit v11 on v10

--- a/solution.py
+++ b/solution.py
@@ -105,7 +105,6 @@
             flip(i, j)
         return carry
 
-    lax.fori_loop(1, row_bands - 1, flip_inner, 0)
 
     zeros_pad = jnp.zeros((PAD, ext_w), jnp.float32)
     for buf in (s0, s1, s2, s3):
@@ -170,6 +169,10 @@
         send(a, 1).start()
 
     def wave(i, carry):
+        @pl.when((i % 2 == 1) & (i <= 2 * (row_bands - 2) - 1))
+        def _():
+            flip_inner((i + 1) // 2, 0)
+
         for k in range(STEPS):
             b = i - k
 

time: 145 us -> 145 us (level)
  no operation moved by 1% of the time
where the time goes in v11:
time: 145 us
  Pallas kernels  71.7 us (49%)
  waiting for transfers between devices  52 us (36%)
  local copies, waits for them, and re-layouts  12.3 us (8%)
  starting transfers between devices  7.67 us (5%)
    pallas_call x1, Pallas kernels, inspect(): pl.pallas_call(functools.partial(inspect_kernel, band_rows, band_cols), o...  71.7 us
    all_to_all x1, waiting for transfers between devices, local(): lax.all_to_all(raw_band.T, 'col', split_axis=0, concat_axis=0, tiled=True)  52 us
    unnamed x7, local copies, waits for them, and re-layouts  12.3 us
    all_to_all x1, starting transfers between devices, local(): lax.all_to_all(raw_band.T, 'col', split_axis=0, concat_axis=0, tiled=True)  7.67 us
  transfers between devices with their start and end apart: 1, of which 1 were waited for; matrix products, arithmetic and copies ran while one was open for 1% of the time, Pallas kernels for 0%

profile of v11, /device:TPU:0, one launch (start us, length us, event | category | flops | bytes accessed | tf_op | source)
XLA Modules:
  0.0 145.1 jit_solution(11156825965946707000)
XLA Ops:
  0.6 5.3 %copy.5 = f32[1024,1024]{0,1:T(8,128)} copy(f32[1024,1024]{1,0:T(8,128)} %param.2) | data formatting | bytes 8388608 | tf_op args[0]
  6.0 0.0 copy-start.1
  6.0 7.7 %all-to-all-start = ((f32[32,32,1024]{2,1,0:T(8,128)}), f32[32,32,1024]{2,1,0:T(8,128)}, u32[]{:S(2)}, u32[]{:S(2)}) async-start(f32[32,32,1024]{2,1,0:T(8,128)} %bitcast.6), calls=%async_computation | async-start | bytes 8388608 | tf_op jit(solution)/shard_map/all_to_all | solution.py:248
  13.7 0.0 copy-done.1
  13.7 0.1 select_reduce_fusion
  13.8 0.7 pad_add_fusion.prm
  14.5 52.0 %all-to-all-done = f32[32,32,1024]{2,1,0:T(8,128)} async-done(((f32[32,32,1024]{2,1,0:T(8,128)}), f32[32,32,1024]{2,1,0:T(8,128)}, u32[]{:S(2)}, u32[]{:S(2)}) %all-to-all-start) | async-done | bytes 4194336 | tf_op jit(solution)/shard_map/all_to_all | solution.py:248
  66.4 71.7 %shard_map.41 = (f32[1024,1024]{1,0:T(8,128)}, f32[1024,1024]{1,0:T(8,128)}) custom-call(s32[8]{0:T(128)} %pad_add_fusion.prm, f32[1024,1024]{1,0:T(8,128)} %bitcast.4.raw_t), custom_call_target="tpu_custom_call" | custom-call | flops 222822400 | bytes 12582912 | tf_op jit(solution)/shard_map/pallas_call | solution.py:217
  138.1 0.0 copy-start
  138.1 4.9 %copy.8 = f32[1024,1024]{1,0:T(8,128)} copy(f32[1024,1024]{1,0:T(8,128)} %get-tuple-element.4) | data formatting | bytes 8388608
  143.0 0.0 copy-done
  143.0 2.0 %copy.9 = f32[1024,1024]{1,0:T(8,128)} copy(f32[1024,1024]{1,0:T(8,128)S(1)} %copy-done) | data formatting | bytes 8388608
  (2 shorter events, 0.0 us)
Async XLA Ops:
  6.0 7.7 %copy-start.1 = (s32[32,2]{0,1:T(2,128)S(1)}, s32[32,2]{0,1:T(2,128)}, u32[]{:S(2)}) copy-start(s32[32,2]{0,1:T(2,128)} %param.3) | copy-start | bytes 772
  6.0 60.5 %all-to-all-start = ((f32[32,32,1024]{2,1,0:T(8,128)}), f32[32,32,1024]{2,1,0:T(8,128)}, u32[]{:S(2)}, u32[]{:S(2)}) async-start(f32[32,32,1024]{2,1,0:T(8,128)} %bitcast.6), calls=%async_computation | async-start | bytes 8388608 | tf_op jit(solution)/shard_map/all_to_all | solution.py:248
  138.1 5.0 %copy-start = (f32[1024,1024]{1,0:T(8,128)S(1)}, f32[1024,1024]{1,0:T(8,128)}, u32[]{:S(2)}) copy-start(f32[1024,1024]{1,0:T(8,128)} %get-tuple-element.5) | copy-start | bytes 12582916
